TPU v7x, 128 devices: a whole 4x4x4 slice. The times are simulated.
128 devices in a mesh: row: 16 (over z, y), col: 8 (over x, core).
Axes of the slice: x: 4, y: 4, z: 4, core: 2. Of those that a mesh axis runs over, the one named last changes fastest.
Arguments:
- features: float32 [16384, 128], P(('row', 'col')), may hold values from -6 to 6
- noise: float32 [16384], P(('row', 'col')), may hold values from 0.05 to 0.5
- owner_slot: int32 [16384], P(('row', 'col')), may hold values from 0 to 16383, as said below
- inv_length: float32 [128], replicated, may hold values from 0.001953125 to 0.03125
Outputs:
- factored: bfloat16 [16384, 16384], P('row', 'col')
Inputs may be any that keep to these rules, and one draw needn't show every extreme that they name: `owner_slot`: A permutation of the storage rows. Storage rows are split into 128 ranges of 128 in order; the 128 samples of range e go to the ranges with the same remainder modulo 8, exactly 8 of them to each such range.
All inputs are finite; a program needn't handle non-finite values.
Results may differ from a plain program's by a relative error of at most 0.0082.
Values may be sent and summed in bfloat16 or wider, within the bound.
No kernel may reach another device: no remote copies, remote signals or barrier semaphores. Data moves between devices by JAX's collectives and lax.ppermute only.
A program may use at most 128 MiB of HBM per device.

v0:
```python
import jax
import jax.numpy as jnp
from jax import lax
from jax.sharding import PartitionSpec as P

NB = 512
PANELS = 2


def spread(shard, axis, root):
    mine = lax.axis_index(axis) == root
    return lax.psum(jnp.where(mine, shard, jnp.zeros_like(shard)), axis)


def to_columns(source):
    ncols = lax.axis_size("col")
    pieces = []
    for halfway in range(2):
        pieces.append(spread(source, "row", lax.axis_index("col") + halfway * ncols))
    stacked = jnp.stack(pieces, axis=0)
    blocks = stacked.shape[1] // NB
    stacked = stacked.reshape(2, blocks, NB, source.shape[1]).transpose(1, 0, 2, 3)
    return stacked.reshape(2 * source.shape[0], source.shape[1])


def global_index(count, groups, place):
    local = jnp.arange(count, dtype=jnp.int32)
    return (local // NB * groups + place) * NB + local % NB


def invert_corner(corner):
    factor = jnp.linalg.cholesky(corner)
    return jax.scipy.linalg.solve_triangular(factor, jnp.eye(NB, dtype=jnp.float32), lower=True)


def kernel_tile(left, right, scale):
    left_sq = jnp.sum(left * left * scale, axis=1)
    right_sq = jnp.sum(right * right * scale, axis=1)
    cross = jnp.einsum("rf,cf->rc", left * scale, right, precision=lax.Precision.HIGHEST)
    return jnp.exp(-0.5 * (left_sq[:, None] + right_sq[None, :] - 2.0 * cross))


def body(features, noise, owner_slot, inv_length):
    nrows = lax.axis_size("row")
    ncols = lax.axis_size("col")
    per_device = features.shape[0]
    per_target = per_device // nrows
    feature_width = features.shape[1]
    target_row = owner_slot // per_device // ncols
    local_slot = owner_slot % per_device
    order = jnp.argsort(target_row * per_device + local_slot, stable=True)
    outgoing = (
        features[order].reshape(nrows, per_target, feature_width),
        noise[order].reshape(nrows, per_target),
        local_slot[order].astype(jnp.float32).reshape(nrows, per_target),
    )
    arrived = (
        lax.all_to_all(
            outgoing[0].astype(jnp.bfloat16), "row", split_axis=0, concat_axis=0, tiled=True
        ).astype(jnp.float32),
        lax.all_to_all(
            outgoing[1].astype(jnp.bfloat16), "row", split_axis=0, concat_axis=0, tiled=True
        ).astype(jnp.float32),
        lax.all_to_all(
            outgoing[2].astype(jnp.bfloat16), "row", split_axis=0, concat_axis=0, tiled=True
        ).astype(jnp.float32),
    )
    placed_at = arrived[2].reshape(per_device).astype(jnp.int32)
    placed = (
        jnp.zeros((per_device, feature_width), jnp.float32)
        .at[placed_at]
        .set(arrived[0].reshape(per_device, feature_width))
    )
    placed_noise = (
        jnp.zeros((per_device,), jnp.float32).at[placed_at].set(arrived[1].reshape(per_device))
    )
    row_feats, row_noise = (
        lax.all_gather(placed.astype(jnp.bfloat16), "col", axis=0, tiled=True),
        lax.all_gather(placed_noise.astype(jnp.bfloat16), "col", axis=0, tiled=True),
    )
    col_feats = to_columns(row_feats)
    row_count = row_feats.shape[0]
    col_count = col_feats.shape[0]
    row_global = global_index(row_count, nrows, lax.axis_index("row"))
    col_global = global_index(col_count, ncols, lax.axis_index("col"))
    row_values = row_feats.astype(jnp.float32)
    col_values = col_feats.astype(jnp.float32)
    matrix = kernel_tile(row_values, col_values, inv_length)
    matrix = matrix + jnp.where(
        row_global[:, None] == col_global[None, :], row_noise.astype(jnp.float32)[:, None], 0.0
    )
    panel_list = []
    for panel_index in range(PANELS):
        corner = spread(matrix[:NB, :NB], "row", panel_index)
        inverse = invert_corner(corner)
        panel = jnp.dot(
            matrix[:, :NB],
            inverse.T,
            precision=lax.Precision.HIGHEST,
            preferred_element_type=jnp.float32,
        )
        panel = jnp.where(row_global[:, None] >= panel_index * NB, panel, 0.0).astype(jnp.bfloat16)
        rows_panel = spread(panel, "col", panel_index)
        cols_panel = to_columns(rows_panel)
        matrix = matrix - jnp.einsum(
            "rk,ck->rc", rows_panel, cols_panel, preferred_element_type=jnp.float32
        )
        panel_list.append(rows_panel)
    width = PANELS * NB
    keep = (row_global[:, None] >= width) & (col_global[None, :] >= width)
    result = jnp.where(keep, matrix, 0.0)
    col_here = lax.axis_index("col")
    for panel_index in range(PANELS):
        leading = jnp.where(
            col_here == panel_index, panel_list[panel_index].astype(jnp.float32), result[:, :NB]
        )
        result = result.at[:, :NB].set(leading)
    return result.astype(jnp.bfloat16)


def solution(mesh):
    in_specs = (P(("row", "col"), None), P(("row", "col")), P(("row", "col")), P())
    out_specs = P("row", "col")
    return jax.shard_map(body, mesh=mesh, in_specs=in_specs, out_specs=out_specs, check_vma=False)
```

profile of v0, /device:TPU:19, one launch (start us, length us, event | category | flops | bytes accessed | tf_op | source)
XLA Modules:
  0.0 975.3 jit_solution(7650948646690895711)
XLA Ops:
  7.3 2.5 sort.17
  11.7 7.7 all-to-all-start
  23.9 5.8 all-to-all-start.1
  29.8 4.4 all-to-all-done.1
  34.3 5.3 all-to-all-start.2
  40.5 15.7 %all_gather.6 = bf16[1024,128]{1,0:T(8,128)(2,1)S(1)} all-gather(bf16[128,128]{1,0:T(8,128)(2,1)S(1)} %convert_element_type.122), channel_id=1, replica_groups=mesh['row'=16,'col'=8] {'col'}, dimensions={0}, use_global_device_ids=true | all-gather | bytes 294912 | tf_op jit(solution)/shard_map/all_gather | solution.py:78
  58.3 8.5 all-gather
  67.7 72.1 %all-reduce.24.cloned.1.call-done = (bf16[1,2,512,128]{3,2,0,1:T(8,128)(2,1)}, bf16[1,2,512,128]{3,2,0,1:T(8,128)(2,1)}) async-done(((bf16[1,2,512,128]{3,2,0,1:T(8,128)(2,1)}, bf16[1,2,512,128]{3,2,0,1:T(8,128)(2,1)}), (bf16[1,2,512,128]{3,2,0,1:T(8,128)(2,1)}, bf16[1,2,512,128]{3,2,0,1:T(8,128)(2,1)})) %all-reduce.24.cloned.1.call-update) | async-done | bytes 524304 | tf_op jit(solution)/shard_map/psum | solution.py:12
  142.2 5.6 select_add_fusion
  147.8 3.2 copy-done.2
  152.5 86.3 %all-reduce.12.cloned.1.call-done = f32[512,512]{0,1:T(8,128)} async-done(((f32[512,512]{0,1:T(8,128)}), f32[512,512]{0,1:T(8,128)}) %all-reduce.12.cloned.1.call-update) | async-done | bytes 1048592 | tf_op jit(solution)/shard_map/psum | solution.py:12
  241.8 11.7 %cholesky.286 = f32[128,128]{1,0:T(8,128)S(1)} custom-call(f32[128,128]{1,0:T(8,128)S(1)} %cholesky.426), custom_call_target="Cholesky" | custom-call | tf_op jit(solution)/shard_map/jit(cholesky)/cholesky | solution.py:32
  253.7 9.8 %custom-call.27 = f32[1,128,128]{1,2,0:T(8,128)S(1)} custom-call(f32[1,128,128]{2,1,0:T(8,128)S(1)} %get-tuple-element.102), custom_call_target="InvertDiagBlocksLowerTriangular" | custom-call | tf_op jit(solution)/shard_map/jit(cholesky)/cholesky | solution.py:32
  264.2 11.7 %cholesky.305 = f32[128,128]{1,0:T(8,128)S(1)} custom-call(f32[128,128]{1,0:T(8,128)S(1)} %cholesky.430), custom_call_target="Cholesky" | custom-call | tf_op jit(solution)/shard_map/jit(cholesky)/cholesky | solution.py:32
  276.0 10.0 %custom-call.28 = f32[1,128,128]{1,2,0:T(8,128)S(1)} custom-call(f32[1,128,128]{2,1,0:T(8,128)S(1)} %get-tuple-element.99), custom_call_target="InvertDiagBlocksLowerTriangular" | custom-call | tf_op jit(solution)/shard_map/jit(cholesky)/cholesky | solution.py:32
  286.6 11.7 %cholesky.326 = f32[128,128]{1,0:T(8,128)S(1)} custom-call(f32[128,128]{1,0:T(8,128)S(1)} %cholesky.435), custom_call_target="Cholesky" | custom-call | tf_op jit(solution)/shard_map/jit(cholesky)/cholesky | solution.py:32
  299.0 9.8 %custom-call.29 = f32[1,128,128]{1,2,0:T(8,128)S(1)} custom-call(f32[1,128,128]{2,1,0:T(8,128)S(1)} %get-tuple-element.96), custom_call_target="InvertDiagBlocksLowerTriangular" | custom-call | tf_op jit(solution)/shard_map/jit(cholesky)/cholesky | solution.py:32
  309.4 11.7 %cholesky.343 = f32[128,128]{1,0:T(8,128)S(1)} custom-call(f32[128,128]{1,0:T(8,128)S(1)} %convolution_subtract_fusion.12), custom_call_target="Cholesky" | custom-call | tf_op jit(solution)/shard_map/jit(cholesky)/cholesky | solution.py:32
  325.4 7.7 while.6
  333.1 39.3 %custom-call.30 = f32[4,128,128]{1,2,0:T(8,128)S(1)} custom-call(f32[4,128,128]{2,1,0:T(8,128)S(1)} %get-tuple-element.47), custom_call_target="InvertDiagBlocksLowerTriangular" | custom-call | tf_op jit(solution)/shard_map/jit(_solve_triangular)/triangular_solve | solution.py:33
  375.6 6.1 fusion.9
  381.8 60.5 %all-reduce.14.cloned.1.call-done = bf16[1024,512]{0,1:T(8,128)(2,1)} async-done(((bf16[1024,512]{0,1:T(8,128)(2,1)}), bf16[1024,512]{0,1:T(8,128)(2,1)}) %all-reduce.14.cloned.1.call-update) | async-done | bytes 1048592 | tf_op jit(solution)/shard_map/psum | solution.py:12
  446.4 91.6 %all-reduce.22.cloned.1.call-done = (bf16[1,2,512,512]{3,2,0,1:T(8,128)(2,1)}, bf16[1,2,512,512]{3,2,0,1:T(8,128)(2,1)}) async-done(((bf16[1,2,512,512]{3,2,0,1:T(8,128)(2,1)}, bf16[1,2,512,512]{3,2,0,1:T(8,128)(2,1)}), (bf16[1,2,512,512]{3,2,0,1:T(8,128)(2,1)}, bf16[1,2,512,512]{3,2,0,1:T(8,128)(2,1)})) %all-reduce.22.cloned.1.call-update) | async-done | bytes 2097168 | tf_op jit(solution)/shard_map/psum | solution.py:12
  538.1 1.7 pad_maximum_fusion
  539.8 5.9 convolution_subtract_fusion
  545.8 3.2 copy-done.3
  550.3 85.9 %all-reduce.16.cloned.1.call-done = f32[512,512]{0,1:T(8,128)} async-done(((f32[512,512]{0,1:T(8,128)}), f32[512,512]{0,1:T(8,128)}) %all-reduce.16.cloned.1.call-update) | async-done | bytes 1048592 | tf_op jit(solution)/shard_map/psum | solution.py:12
  640.3 11.7 %cholesky.358 = f32[128,128]{1,0:T(8,128)S(1)} custom-call(f32[128,128]{1,0:T(8,128)S(1)} %cholesky.439), custom_call_target="Cholesky" | custom-call | tf_op jit(solution)/shard_map/jit(cholesky)/cholesky | solution.py:32
  652.1 9.8 %custom-call.31 = f32[1,128,128]{1,2,0:T(8,128)S(1)} custom-call(f32[1,128,128]{2,1,0:T(8,128)S(1)} %get-tuple-element.92), custom_call_target="InvertDiagBlocksLowerTriangular" | custom-call | tf_op jit(solution)/shard_map/jit(cholesky)/cholesky | solution.py:32
  664.5 11.7 %cholesky.377 = f32[128,128]{1,0:T(8,128)S(1)} custom-call(f32[128,128]{1,0:T(8,128)S(1)} %cholesky.443), custom_call_target="Cholesky" | custom-call | tf_op jit(solution)/shard_map/jit(cholesky)/cholesky | solution.py:32
  677.5 10.0 %custom-call.32 = f32[1,128,128]{1,2,0:T(8,128)S(1)} custom-call(f32[1,128,128]{2,1,0:T(8,128)S(1)} %get-tuple-element.89), custom_call_target="InvertDiagBlocksLowerTriangular" | custom-call | tf_op jit(solution)/shard_map/jit(cholesky)/cholesky | solution.py:32
  689.1 11.7 %cholesky.398 = f32[128,128]{1,0:T(8,128)S(1)} custom-call(f32[128,128]{1,0:T(8,128)S(1)} %cholesky.448), custom_call_target="Cholesky" | custom-call | tf_op jit(solution)/shard_map/jit(cholesky)/cholesky | solution.py:32
  701.5 9.8 %custom-call.33 = f32[1,128,128]{1,2,0:T(8,128)S(1)} custom-call(f32[1,128,128]{2,1,0:T(8,128)S(1)} %get-tuple-element.86), custom_call_target="InvertDiagBlocksLowerTriangular" | custom-call | tf_op jit(solution)/shard_map/jit(cholesky)/cholesky | solution.py:32
  712.7 11.7 %cholesky.415 = f32[128,128]{1,0:T(8,128)S(1)} custom-call(f32[128,128]{1,0:T(8,128)S(1)} %convolution_subtract_fusion.11), custom_call_target="Cholesky" | custom-call | tf_op jit(solution)/shard_map/jit(cholesky)/cholesky | solution.py:32
  729.1 11.2 %while.7 = (s32[]{:T(128)}, f32[512,512]{1,0:T(8,128)}, s32[4,2]{0,1:T(2,128)S(1)}, f32[4,128,128]{2,1,0:T(8,128)S(1)}, s32[]{:T(128)}) while((s32[]{:T(128)}, f32[512,512]{1,0:T(8,128)}, s32[4,2]{0,1:T(2,128)S(1)}, f32[4,128,128]{2,1,0:T(8,128)S(1)}, s32[]{:T(128)}) %tuple.86), condition=%wide.while_cond.2.clone, body=%wide.while_body.2.clone.sunk | while | flops 2 | bytes 131181 | solution.py:33
  729.7 2.2 bitcast_dynamic-update-slice_fusion.5
  732.5 2.2 bitcast_dynamic-update-slice_fusion.5
  735.3 2.2 bitcast_dynamic-update-slice_fusion.5
  738.1 2.1 bitcast_dynamic-update-slice_fusion.5
  740.3 39.3 %custom-call.34 = f32[4,128,128]{1,2,0:T(8,128)S(1)} custom-call(f32[4,128,128]{2,1,0:T(8,128)S(1)} %get-tuple-element.48), custom_call_target="InvertDiagBlocksLowerTriangular" | custom-call | tf_op jit(solution)/shard_map/jit(_solve_triangular)/triangular_solve | solution.py:33
  785.4 6.1 fusion.12
  791.6 60.4 %all-reduce.18.cloned.1.call-done = bf16[1024,512]{0,1:T(8,128)(2,1)} async-done(((bf16[1024,512]{0,1:T(8,128)(2,1)}), bf16[1024,512]{0,1:T(8,128)(2,1)}) %all-reduce.18.cloned.1.call-update) | async-done | bytes 1048592 | tf_op jit(solution)/shard_map/psum | solution.py:12
  856.8 90.9 %all-reduce.20.cloned.1.call-done = (bf16[1,2,512,512]{3,2,0,1:T(8,128)(2,1)}, bf16[1,2,512,512]{3,2,0,1:T(8,128)(2,1)}) async-done(((bf16[1,2,512,512]{3,2,0,1:T(8,128)(2,1)}, bf16[1,2,512,512]{3,2,0,1:T(8,128)(2,1)}), (bf16[1,2,512,512]{3,2,0,1:T(8,128)(2,1)}, bf16[1,2,512,512]{3,2,0,1:T(8,128)(2,1)})) %all-reduce.20.cloned.1.call-update) | async-done | bytes 2097168 | tf_op jit(solution)/shard_map/psum | solution.py:12
  949.4 4.9 subtract_select_fusion
  954.4 1.9 copy.86
  956.3 3.2 fusion.15
  959.5 2.3 fusion
  961.8 6.4 copy.38
  (152 shorter events, 66.6 us)
Async XLA Ops:
  6.5 13.0 %copy-start = (f32[128,128]{1,0:T(8,128)S(1)}, f32[128,128]{1,0:T(8,128)}, u32[]{:S(2)}) copy-start(f32[128,128]{1,0:T(8,128)} %param.11) | copy-start | bytes 196612
  6.5 135.2 %copy-start.7 = (f32[128]{0:T(128)S(1)}, f32[128]{0:T(128)}, u32[]{:S(2)}) copy-start(f32[128]{0:T(128)} %param.14) | copy-start | bytes 1540
  11.7 12.2 %all-to-all-start = ((bf16[16,1,8]{2,1,0:T(2,128)(2,1)}), bf16[16,1,8]{2,1,0:T(2,128)(2,1)S(1)}, u32[]{:S(2)}, u32[]{:S(2)}) async-start(bf16[16,1,8]{2,1,0:T(2,128)(2,1)} %convert_element_type.139), calls=%async_computation | async-start | bytes 16384 | tf_op jit(solution)/shard_map/all_to_all | solution.py:64
  23.9 10.4 %all-to-all-start.1 = ((bf16[16,8,128]{2,1,0:T(8,128)(2,1)}), bf16[16,8,128]{2,1,0:T(8,128)(2,1)S(1)}, u32[]{:S(2)}, u32[]{:S(2)}) async-start(bf16[16,8,128]{2,1,0:T(8,128)(2,1)} %bitcast.101), calls=%async_computation.1 | async-start | bytes 65536 | tf_op jit(solution)/shard_map/all_to_all | solution.py:58
  34.3 22.9 %all-to-all-start.2 = ((bf16[16,1,8]{2,1,0:T(2,128)(2,1)}), bf16[16,1,8]{2,1,0:T(2,128)(2,1)S(1)}, u32[]{:S(2)}, u32[]{:S(2)}) async-start(bf16[16,1,8]{2,1,0:T(2,128)(2,1)} %convert_element_type.140), calls=%async_computation.2 | async-start | bytes 16384 | tf_op jit(solution)/shard_map/all_to_all | solution.py:61
  39.5 100.3 %all-reduce.24.cloned.1.call-start = ((), (), s32[]{:S(2)}) async-start(), calls=%async_computation.9 | async-start | bytes 1048576 | tf_op jit(solution)/shard_map/psum | solution.py:12
  57.1 181.7 %all-reduce.12.cloned.1.call-start = ((), (), s32[]{:S(2)}) async-start(), calls=%async_computation.3 | async-start | bytes 2097152 | tf_op jit(solution)/shard_map/psum | solution.py:12
  147.8 3.2 copy-start.2
  152.1 290.2 %all-reduce.14.cloned.1.call-start = ((), (), s32[]{:S(2)}) async-start(), calls=%async_computation.4 | async-start | bytes 2097152 | tf_op jit(solution)/shard_map/psum | solution.py:12
  381.8 156.3 %all-reduce.22.cloned.1.call-start = ((), (), s32[]{:S(2)}) async-start(), calls=%async_computation.8 | async-start | bytes 4194304 | tf_op jit(solution)/shard_map/psum | solution.py:12
  445.0 94.8 %copy-start.4 = (bf16[1024,512]{0,1:T(8,128)(2,1)S(1)}, bf16[1024,512]{0,1:T(8,128)(2,1)}, u32[]{:S(2)}) copy-start(bf16[1024,512]{0,1:T(8,128)(2,1)} %all-reduce.14.cloned.1.call-done) | copy-start | bytes 3145732
  446.4 189.9 %all-reduce.16.cloned.1.call-start = ((), (), s32[]{:S(2)}) async-start(), calls=%async_computation.5 | async-start | bytes 2097152 | tf_op jit(solution)/shard_map/psum | solution.py:12
  545.7 3.2 copy-start.3
  550.1 301.9 %all-reduce.18.cloned.1.call-start = ((), (), s32[]{:S(2)}) async-start(), calls=%async_computation.6 | async-start | bytes 2097152 | tf_op jit(solution)/shard_map/psum | solution.py:12
  639.3 1.0 copy-start.6
  791.6 156.1 %all-reduce.20.cloned.1.call-start = ((), (), s32[]{:S(2)}) async-start(), calls=%async_computation.7 | async-start | bytes 4194304 | tf_op jit(solution)/shard_map/psum | solution.py:12
  854.7 94.7 %copy-start.5 = (bf16[1024,512]{0,1:T(8,128)(2,1)S(1)}, bf16[1024,512]{0,1:T(8,128)(2,1)}, u32[]{:S(2)}) copy-start(bf16[1024,512]{0,1:T(8,128)(2,1)} %all-reduce.18.cloned.1.call-done) | copy-start | bytes 3145732
  959.5 8.7 copy-start.1
Sparse Core Ops, SparseCore 0:
  57.2 82.5 all-reduce.23
  152.2 86.5 all-reduce.11
  381.9 60.3 all-reduce.13
  446.5 91.5 all-reduce.21
  550.2 86.0 all-reduce.15
  791.7 60.2 all-reduce.17
  856.2 91.4 all-reduce.19
where the time goes:
time: 987 us; the launch traced here: 975 us
  waiting for transfers between devices  553 us (56%)
  other arithmetic  262 us (27%)
  local copies, waits for them, and re-layouts  51.8 us (5%)
  matrix products  45 us (5%)
  blocking collectives  24.2 us (2%)
  between operations  19.6 us (2%)
  starting transfers between devices  19.4 us (2%)
    psum x7, waiting for transfers between devices, spread(): return lax.psum(jnp.where(mine, shard, jnp.zeros_like(shard)), axis)  548 us
    another operation x29, other arithmetic, invert_corner(): factor = jnp.linalg.cholesky(corner)  158 us
    another operation x5, other arithmetic, invert_corner(): jax.scipy.linalg.solve_triangular(factor, jnp.eye(NB, dtype=jnp.float32),...  80.2 us
  transfers between devices with their start and end apart: 10, of which 9 were waited for; matrix products, arithmetic and copies ran while one was open for 1% of the time, Pallas kernels for 0%

commit v1 on v0

v1 whole, which is shorter than its diff:
```python
import jax
import jax.numpy as jnp
from jax import lax
from jax.experimental import pallas as pl
from jax.experimental.pallas import tpu as pltpu
from jax.sharding import PartitionSpec as P

NB = 512
PANELS = 2
F = 128
f32 = jnp.float32
bf16 = jnp.bfloat16


def split3(x):
    h = x.astype(bf16)
    r = x - h.astype(f32)
    m = r.astype(bf16)
    return h, m, (r - m.astype(f32)).astype(bf16)


def left6(pieces):
    h, m, l = pieces
    return jnp.concatenate([h, h, m, m, h, l], axis=1)


def right6(pieces, axis):
    h, m, l = pieces
    return jnp.concatenate([h, m, h, m, l, h], axis=axis)


def nt(x, y):
    return lax.dot_general(x, y, (((1,), (1,)), ((), ())), preferred_element_type=f32)


def nn(x, y):
    return lax.dot_general(x, y, (((1,), (0,)), ((), ())), preferred_element_type=f32)


def iota(shape, dim):
    return lax.broadcasted_iota(jnp.int32, shape, dim)


def pack_kernel(feat_ref, noise_ref, slot_col_ref, slot_row_ref, sorted_ref, extra_ref):
    n = feat_ref.shape[0]
    col = slot_col_ref[...]
    row = slot_row_ref[...]
    before = (row < col).astype(f32)
    rank_col = jnp.sum(before, axis=1, keepdims=True).astype(jnp.int32)
    rank_row = jnp.sum((col < row).astype(f32), axis=0, keepdims=True).astype(jnp.int32)
    pick = (iota((n, n), 0) == rank_row).astype(bf16)
    sorted_ref[...] = nn(pick, feat_ref[...].astype(bf16)).astype(bf16)
    back = rank_col == iota((n, n), 1)
    slots = jnp.sum(jnp.where(back, (col % n).astype(f32), 0.0), axis=0, keepdims=True)
    noises = jnp.sum(
        jnp.where(back, noise_ref[...].astype(bf16).astype(f32), 0.0), axis=0, keepdims=True
    )
    which = iota((8, n), 0)
    extra_ref[...] = jnp.where(which == 0, slots, jnp.where(which == 1, noises, 0.0)).astype(bf16)


def spread_rows(table, target):
    n = table.shape[0]
    lane = iota((n, n), 1)
    mine = jnp.where(lane // 8 == target, table, jnp.zeros_like(table))
    comb = (iota((n, n), 0) % 8 == iota((n, n), 1) % 8).astype(bf16)
    spread = nn(mine, comb).reshape(n // 8, 8, n)
    take = iota((n // 8, 8, n), 2) // 8 == iota((n // 8, 8, n), 0)
    return jnp.sum(jnp.where(take, spread, 0.0), axis=0)


def place_range(slots, noises, samples):
    n = samples.shape[0]
    hot = iota((n, n), 0).astype(f32) == slots
    rows = nn(hot.astype(bf16), samples).astype(bf16)
    noise = jnp.sum(jnp.where(hot, noises, 0.0), axis=1, keepdims=True)
    return rows, noise


def fill_lanes(values, width):
    lane = iota((values[0].shape[0], width), 1)
    out = jnp.zeros((values[0].shape[0], width), f32)
    for i, v in enumerate(values):
        out = jnp.where(lane == i, v, out)
    return out.astype(bf16)


def half_norm(x, scale):
    return -0.5 * jnp.sum(x * x * scale, axis=1, keepdims=True)


def left_operand(rows, scale):
    h, m, l = split3(half_norm(rows.astype(f32), scale))
    extra = fill_lanes([1.0 + 0.0 * h.astype(f32)] * 3 + [h.astype(f32), m.astype(f32), l.astype(f32)], F)
    return jnp.concatenate([rows, rows, rows, extra], axis=1)


def right_operand(rows, scale):
    x = rows.astype(f32)
    h, m, l = split3(half_norm(x, scale))
    extra = fill_lanes([h.astype(f32), m.astype(f32), l.astype(f32)] + [1.0 + 0.0 * h.astype(f32)] * 3, F)
    return jnp.concatenate([*split3(x * scale), extra], axis=1)


def add_diagonal(value, noise):
    n = value.shape[0]
    return value + jnp.where(iota((n, n), 0) == iota((n, n), 1), noise, 0.0)


def lane(x, j):
    return jnp.broadcast_to(x[:, j : j + 1], (8, 128))


def sub(x, k):
    return jnp.broadcast_to(x[k : k + 1, :], (8, 128))


def invert_factor(block):
    ri = iota((8, 128), 0)
    ci = iota((8, 128), 1)
    a = [block[8 * i : 8 * i + 8, :] for i in range(16)]
    b = [(ri + 8 * i == ci).astype(f32) for i in range(16)]
    out = []
    for g in range(16):
        cb = [lane(a[g], 8 * g + k) for k in range(8)]
        d = [[sub(cb[k], r) if r >= k else None for k in range(8)] for r in range(8)]
        ar = [sub(a[g], k) for k in range(8)]
        br = [sub(b[g], k) for k in range(8)]
        more = g + 1 < 16
        cc = [lane(a[g + 1], 8 * g + k) for k in range(8)] if more else None
        rs = [None] * 8
        l = [[None] * 8 for _ in range(8)]
        for k in range(8):
            rs[k] = lax.rsqrt(d[k][k])
            for m in range(k + 1, 8):
                l[m][k] = d[m][k] * rs[k]
            for m in range(k + 1, 8):
                for j in range(k + 1, m + 1):
                    d[m][j] = d[m][j] - l[m][k] * l[j][k]
            ar[k] = ar[k] * rs[k]
            br[k] = br[k] * rs[k]
            if more:
                cc[k] = cc[k] * rs[k]
            for m in range(k + 1, 8):
                ar[m] = ar[m] - l[m][k] * ar[k]
                br[m] = br[m] - l[m][k] * br[k]
                if more:
                    cc[m] = cc[m] - l[m][k] * cc[k]
            if more:
                a[g + 1] = a[g + 1] - cc[k] * ar[k]
                b[g + 1] = b[g + 1] - cc[k] * br[k]
        v = br[7]
        for k in range(7):
            v = jnp.where(ri == k, br[k], v)
        out.append(v)
        if g + 2 < 16:
            z = [None] * 8
            y = [None] * 8
            for k in range(7, -1, -1):
                zz = ar[k]
                yy = br[k]
                for m in range(7, k, -1):
                    zz = zz - l[m][k] * z[m]
                    yy = yy - l[m][k] * y[m]
                z[k] = zz * rs[k]
                y[k] = yy * rs[k]
            for i in range(g + 2, 16):
                ai = a[i]
                bi = b[i]
                for k in range(8):
                    c = lane(a[i], 8 * g + k)
                    ai = ai - c * z[k]
                    bi = bi - c * y[k]
                a[i] = ai
                b[i] = bi
    return jnp.concatenate(out, axis=0)


def invert_panel(a_ref, w_ref):
    w_ref[...] = jnp.zeros((NB, NB), f32)
    for s in range(0, NB, 128):
        e = s + 128
        w = invert_factor(a_ref[s:e, s:e])
        pieces = split3(w)
        wl = left6(pieces)
        if e < NB:
            low = nt(left6(split3(a_ref[e:NB, s:e])), right6(pieces, 1))
            low_pieces = split3(low)
            low_left = left6(low_pieces)
            a_ref[e:NB, e:NB] = a_ref[e:NB, e:NB] - nt(low_left, right6(low_pieces, 1))
        if s > 0:
            w_ref[s:e, 0:s] = nn(wl, right6(split3(w_ref[s:e, 0:s]), 0))
        w_ref[s:e, s:e] = w
        if e < NB:
            w_ref[e:NB, 0:e] = w_ref[e:NB, 0:e] - nn(low_left, right6(split3(w_ref[s:e, 0:e]), 0))


def times_inverse(left, pieces):
    half = NB // 2
    lp = split3(left)
    top = nt(
        left6([p[:, :half] for p in lp]), right6([p[:half, :half] for p in pieces], 1)
    )
    bottom = nt(left6(lp), right6([p[half:, :] for p in pieces], 1))
    return jnp.concatenate([top, bottom], axis=1)


def factor_kernel(
    place_ref, samples_ref, slot_ref, noise_ref, scale_ref,
    right_ref, lead_noise_ref, w_ref, p21_ref, slots_ref, noises_ref, a_ref, inv_ref,
):
    scale = scale_ref[...]
    slot_table = slot_ref[...]
    noise_table = noise_ref[...]
    for panel in range(PANELS):
        slots = spread_rows(slot_table, panel)
        noises = spread_rows(noise_table, panel)
        rows = []
        for i in range(4):
            placed, noise = place_range(
                slots[i : i + 1, :], noises[i : i + 1, :], samples_ref[panel * 4 + i]
            )
            rows.append(placed)
            lead_noise_ref[panel * NB + i * 128 : panel * NB + (i + 1) * 128, :] = noise
        rows = jnp.concatenate(rows, axis=0)
        right_ref[panel * NB : (panel + 1) * NB, :] = right_operand(rows, scale)
        left = left_operand(rows, scale)
        for other in range(panel + 1):
            value = jnp.exp(nt(left, right_ref[other * NB : (other + 1) * NB, :]))
            if other == panel:
                value = add_diagonal(value, lead_noise_ref[panel * NB : (panel + 1) * NB, :])
            a_ref[panel + other] = value

    for kind in range(3):
        slots_ref[kind] = spread_rows(slot_table, place_ref[kind])
        noises_ref[kind] = spread_rows(noise_table, place_ref[kind])

    def one_panel(panel, carry):
        invert_panel(a_ref.at[0], inv_ref)
        pieces = split3(inv_ref[...])
        for i in range(3):
            w_ref[panel, i] = pieces[i]

        @pl.when(panel == 0)
        def _():
            p21 = times_inverse(a_ref[1], pieces).astype(bf16)
            p21_ref[...] = p21
            a_ref[0] = a_ref[2] - nt(p21, p21)

        return carry

    lax.fori_loop(0, PANELS, one_panel, 0)


def panel_kernel(
    block_ref, samples_ref, slots_ref, noises_ref, scale_ref, right_ref, lead_noise_ref,
    w_ref, p21_ref, rows_ref, noise_ref, p_ref,
):
    step = pl.program_id(0)
    kind = jnp.where(step < 2, 0, 1 + step % 2)
    first = 4 * jnp.where(step < 2, step, (step - 2) // 2)
    block = block_ref[step]
    rows = []
    for i in range(4):
        placed, noise = place_range(
            slots_ref[kind, pl.ds(first + i, 1), :],
            noises_ref[kind, pl.ds(first + i, 1), :],
            samples_ref[0, i],
        )
        rows.append(placed)
        noise_ref[i * 128 : (i + 1) * 128, :] = noise
    rows = jnp.concatenate(rows, axis=0)
    rows_ref[...] = rows
    left = left_operand(rows, scale_ref[...])
    columns = []
    for panel in range(PANELS):
        value = jnp.exp(nt(left, right_ref[panel * NB : (panel + 1) * NB, :]))
        lead = jnp.where(block == panel, lead_noise_ref[panel * NB : (panel + 1) * NB, :], 0.0)
        columns.append(add_diagonal(value, lead))
    p1 = times_inverse(columns[0], [w_ref[0, i] for i in range(3)]).astype(bf16)
    p_ref[:, :NB] = p1
    second = columns[1] - nt(p1, p21_ref[...])
    p2 = times_inverse(second, [w_ref[1, i] for i in range(3)])
    p_ref[:, NB:] = jnp.where(block >= 1, p2, 0.0).astype(bf16)


def tile_kernel(
    block_ref, left_rows_ref, right_rows_ref, noise_ref, scale_ref, p_left_ref, p_right_ref,
    out_ref, right_ref,
):
    row_block = block_ref[pl.program_id(1)]
    col_block = block_ref[2 + pl.program_id(0)]

    @pl.when(pl.program_id(1) == 0)
    def _():
        right_ref[...] = right_operand(right_rows_ref[...], scale_ref[...])

    @pl.when(col_block < PANELS)
    def _():
        out_ref[...] = jnp.where(col_block == 0, p_left_ref[:, :NB], p_left_ref[:, NB:])

    @pl.when((col_block >= PANELS) & (row_block < PANELS))
    def _():
        out_ref[...] = jnp.zeros(out_ref.shape, bf16)

    @pl.when((col_block >= PANELS) & (row_block >= PANELS))
    def _():
        left = left_operand(left_rows_ref[...], scale_ref[...])
        value = jnp.exp(nt(left, right_ref[...]))
        noise = jnp.where(row_block == col_block, noise_ref[...], 0.0)
        value = add_diagonal(value, noise) - nt(p_left_ref[...], p_right_ref[...])
        out_ref[...] = value.astype(bf16)


VMEM = pl.BlockSpec(memory_space=pltpu.VMEM)
SMEM = pl.BlockSpec(memory_space=pltpu.SMEM)
PARAMS = pltpu.CompilerParams(vmem_limit_bytes=56 * 1024 * 1024)


def body(features, noise, owner_slot, inv_length):
    nrows = lax.axis_size("row")
    ncols = lax.axis_size("col")
    here = features.shape[0]
    count = nrows * ncols
    r = lax.axis_index("row").astype(jnp.int32)
    c = lax.axis_index("col").astype(jnp.int32)
    scale = inv_length.reshape(1, F)

    arranged, extra = pl.pallas_call(
        pack_kernel,
        out_shape=(
            jax.ShapeDtypeStruct((here, F), bf16),
            jax.ShapeDtypeStruct((8, here), bf16),
        ),
        in_specs=[VMEM] * 4,
        out_specs=(VMEM, VMEM),
        name="pack",
    )(features, noise.reshape(here, 1), owner_slot.reshape(here, 1), owner_slot.reshape(1, here))

    lead_send = jnp.concatenate([arranged[:16], extra], axis=0)
    lead_send = jnp.broadcast_to(lead_send[None], (count, 24, F))
    lead = lax.all_to_all(lead_send, ("row", "col"), 0, 0, tiled=True)

    groups = arranged.reshape(nrows, 8, F)
    to_row = jnp.broadcast_to(groups[:, None], (nrows, ncols, 8, F))
    to_col = jnp.broadcast_to(groups.reshape(1, 2, ncols, 8, F), (nrows, 2, ncols, 8, F))
    bulk_send = jnp.concatenate([to_row, to_col[:, 0], to_col[:, 1]], axis=2)
    bulk_send = bulk_send.reshape(count, 24, F)
    bulk_send, lead = lax.optimization_barrier((bulk_send, lead))
    bulk = lax.all_to_all(bulk_send, ("row", "col"), 0, 0, tiled=True)

    lead_samples = lead.reshape(nrows, ncols, 24, F)[:, :4, :16].reshape(nrows, 4, 2, 8, F)
    lead_samples = lead_samples.transpose(2, 1, 0, 3, 4).reshape(8, here, F)
    place = jnp.stack([r, c, c + ncols])
    blocks = jnp.stack([r, r + nrows, c, c + ncols, c + 2 * ncols, c + 3 * ncols])

    right, lead_noise, w, p21, slots, noises = pl.pallas_call(
        factor_kernel,
        out_shape=(
            jax.ShapeDtypeStruct((PANELS * NB, 4 * F), bf16),
            jax.ShapeDtypeStruct((PANELS * NB, 1), f32),
            jax.ShapeDtypeStruct((PANELS, 3, NB, NB), bf16),
            jax.ShapeDtypeStruct((NB, NB), bf16),
            jax.ShapeDtypeStruct((3, 8, here), f32),
            jax.ShapeDtypeStruct((3, 8, here), f32),
        ),
        in_specs=[SMEM] + [VMEM] * 4,
        out_specs=(VMEM,) * 6,
        scratch_shapes=[pltpu.VMEM((3, NB, NB), f32), pltpu.VMEM((NB, NB), f32)],
        compiler_params=PARAMS,
        name="factor",
    )(place, lead_samples, lead[:, 16], lead[:, 17], scale)

    bulk_samples = bulk.reshape(nrows, ncols, 3, 8, F).transpose(2, 1, 0, 3, 4)
    bulk_samples = bulk_samples.reshape(3, ncols, here, F)

    def kind_of(i):
        return jnp.where(i < 2, 0, 1 + i % 2), jnp.where(i < 2, i, (i - 2) // 2)

    whole = lambda *shape: pl.BlockSpec(shape, lambda i, b: (0,) * len(shape))
    rows, row_noise, panels = pl.pallas_call(
        panel_kernel,
        grid_spec=pltpu.PrefetchScalarGridSpec(
            num_scalar_prefetch=1,
            grid=(6,),
            in_specs=[
                pl.BlockSpec((1, 4, here, F), lambda i, b: (*kind_of(i), 0, 0)),
                whole(3, 8, here),
                whole(3, 8, here),
                whole(1, F),
                whole(PANELS * NB, 4 * F),
                whole(PANELS * NB, 1),
                whole(PANELS, 3, NB, NB),
                whole(NB, NB),
            ],
            out_specs=[
                pl.BlockSpec((NB, F), lambda i, b: (i, 0)),
                pl.BlockSpec((NB, 1), lambda i, b: (i, 0)),
                pl.BlockSpec((NB, PANELS * NB), lambda i, b: (i, 0)),
            ],
        ),
        out_shape=(
            jax.ShapeDtypeStruct((6 * NB, F), bf16),
            jax.ShapeDtypeStruct((6 * NB, 1), f32),
            jax.ShapeDtypeStruct((6 * NB, PANELS * NB), bf16),
        ),
        compiler_params=PARAMS,
        name="panel_rows",
    )(blocks, bulk_samples, slots, noises, scale, right, lead_noise, w, p21)

    return pl.pallas_call(
        tile_kernel,
        grid_spec=pltpu.PrefetchScalarGridSpec(
            num_scalar_prefetch=1,
            grid=(4, 2),
            in_specs=[
                pl.BlockSpec((NB, F), lambda j, i, b: (i, 0)),
                pl.BlockSpec((NB, F), lambda j, i, b: (2 + j, 0)),
                pl.BlockSpec((NB, 1), lambda j, i, b: (i, 0)),
                pl.BlockSpec((1, F), lambda j, i, b: (0, 0)),
                pl.BlockSpec((NB, PANELS * NB), lambda j, i, b: (i, 0)),
                pl.BlockSpec((NB, PANELS * NB), lambda j, i, b: (2 + j, 0)),
            ],
            out_specs=pl.BlockSpec((NB, NB), lambda j, i, b: (i, j)),
            scratch_shapes=[pltpu.VMEM((NB, 4 * F), bf16)],
        ),
        out_shape=jax.ShapeDtypeStruct((2 * NB, 4 * NB), bf16),
        compiler_params=PARAMS,
        name="tiles",
    )(blocks, rows, rows, row_noise, scale, panels, panels)


def solution(mesh):
    in_specs = (P(("row", "col"), None), P(("row", "col")), P(("row", "col")), P())
    out_specs = P("row", "col")
    return jax.shard_map(body, mesh=mesh, in_specs=in_specs, out_specs=out_specs, check_vma=False)
```

time: 987 us -> 136 us (0.14); the launches traced: 975 us -> 136 us
  waiting for transfers between devices: 553 us -> 12.2 us
  other arithmetic: 262 us -> 2.34 us
  Pallas kernels: 0 us -> 94.7 us
  matrix products: 45 us -> 0 us
  local copies, waits for them, and re-layouts: 51.8 us -> 7.98 us
  blocking collectives: 24.2 us -> 0 us
  between operations: 19.6 us -> 0.09 us
    psum x7 -> x0, waiting for transfers between devices: 548 us -> none  [spread(): return lax.psum(jnp.where(mine, shard, jnp.zeros_like(shard)), axis)]
    another operation x37 -> x1, other arithmetic: 242 us -> 0.66 us  [body(): place = jnp.stack([r, c, c + ncols])]
    pallas_call x0 -> x4, Pallas kernels: none -> 94.7 us  [the longest x1 47.9 us: body(): pl.pallas_call(factor_kernel, out_shape=(jax.ShapeDtypeStruct((PANELS * N...]
    dot_general x5 -> x0, matrix products: 28.8 us -> none  [the longest x2 12.2 us: body(): jnp.dot(matrix[:, :NB], inverse.T, precision=lax.Precision.HIGHEST, prefe...]
    another operation x40 -> x1, local copies, waits for them, and re-layouts: 25.4 us -> 0.69 us  [body(): jnp.stack([r, r + nrows, c, c + ncols, c + 2 * ncols, c + 3 * ncols])]
    all_gather x2 -> x0, blocking collectives: 24.2 us -> none  [the longest x1 15.7 us: body(): lax.all_gather(placed.astype(jnp.bfloat16), 'col', axis=0, tiled=True)]
    another operation x26 -> x0, matrix products: 16.2 us -> none  [the longest x14 8.89 us: invert_corner(): jax.scipy.linalg.solve_triangular(factor, jnp.eye(NB, dtype=jnp.float32),...]
    unnamed x19 -> x2, local copies, waits for them, and re-layouts: 10.3 us -> 0.01 us
  transfers between devices with their start and end apart: 10 -> 2, of which waited for: 9 -> 1; matrix products, arithmetic and copies ran while one was open for 1% -> 3% of each run, Pallas kernels for 0% -> 35%
where the time goes in v1:
time: 136 us
  Pallas kernels  94.7 us (70%)
  starting transfers between devices  18.2 us (13%)
  waiting for transfers between devices  12.2 us (9%)
  local copies, waits for them, and re-layouts  7.98 us (6%)
  other arithmetic  2.34 us (2%)
    pallas_call x1, Pallas kernels, body(): pl.pallas_call(factor_kernel, out_shape=(jax.ShapeDtypeStruct((PANELS * N...  47.9 us
    pallas_call x1, Pallas kernels, body(): pl.pallas_call(panel_kernel, grid_spec=pltpu.PrefetchScalarGridSpec(num_s...  29.9 us
    pallas_call x1, Pallas kernels, body(): pl.pallas_call(tile_kernel, grid_spec=pltpu.PrefetchScalarGridSpec(num_sc...  15.3 us
    all_to_all x1, waiting for transfers between devices, body(): lead = lax.all_to_all(lead_send, ('row', 'col'), 0, 0, tiled=True)  12.2 us
    all_to_all x1, starting transfers between devices, body(): lead = lax.all_to_all(lead_send, ('row', 'col'), 0, 0, tiled=True)  10.6 us
    all_to_all x1, starting transfers between devices, body(): bulk = lax.all_to_all(bulk_send, ('row', 'col'), 0, 0, tiled=True)  7.53 us
  transfers between devices with their start and end apart: 2, of which 1 were waited for; matrix products, arithmetic and copies ran while one was open for 3% of the time, Pallas kernels for 35%

profile of v1, /device:TPU:19, one launch (start us, length us, event | category | flops | bytes accessed | tf_op | source)
XLA Modules:
  0.0 135.6 jit_solution(8762392459562894944)
XLA Ops:
  0.0 1.4 %copy.17.noise_ref = f32[128,1]{1,0:T(8,128)} copy(f32[128,1]{0,1:T(1,128)} %bitcast.47) | data formatting | bytes 1024 | tf_op jit(solution)/shard_map/reshape | solution.py:338
  1.4 1.4 %copy.18.slot_col_ref = s32[128,1]{1,0:T(8,128)} copy(s32[128,1]{0,1:T(1,128)} %bitcast.45) | data formatting | bytes 1024 | tf_op jit(solution)/shard_map/reshape | solution.py:338
  2.8 1.7 %pack.1 = (bf16[128,128]{1,0:T(8,128)(2,1)}, bf16[8,128]{1,0:T(8,128)(2,1)}) custom-call(f32[128,128]{1,0:T(8,128)} %feat_ref.1, f32[128,1]{1,0:T(8,128)} %copy.17.noise_ref, s32[128,1]{1,0:T(8,128)} %copy.18.slot_col_ref, s32[1,128]{1,0:T(1,128)} %bitcast.46), custom_call_target="tpu_custom_call" | custom-call | tf_op jit(solution)/shard_map/pack/pallas_call | solution.py:329
  4.5 0.0 copy-start
  4.5 0.7 slice.24
  5.2 0.7 pad_maximum_fusion.1
  5.9 1.0 broadcast_in_dim.30
  6.9 10.6 %all-to-all-start = ((bf16[128,24,128]{2,1,0:T(8,128)(2,1)}), bf16[128,24,128]{2,1,0:T(8,128)(2,1)S(1)}, u32[]{:S(2)}, u32[]{:S(2)}) async-start(bf16[128,24,128]{2,1,0:T(8,128)(2,1)} %broadcast_in_dim.30), calls=%async_computation | async-start | bytes 1572864 | tf_op jit(solution)/shard_map/all_to_all | solution.py:342
  17.5 0.0 copy-done
  17.7 1.0 pad_maximum_fusion
  18.7 12.2 %all-to-all-done = bf16[128,24,128]{2,1,0:T(8,128)(2,1)S(1)} async-done(((bf16[128,24,128]{2,1,0:T(8,128)(2,1)}), bf16[128,24,128]{2,1,0:T(8,128)(2,1)S(1)}, u32[]{:S(2)}, u32[]{:S(2)}) %all-to-all-start) | async-done | bytes 786464 | tf_op jit(solution)/shard_map/all_to_all | solution.py:342
  31.0 7.5 %all-to-all-start.1 = ((bf16[128,24,128]{2,1,0:T(8,128)(2,1)}), bf16[128,24,128]{2,1,0:T(8,128)(2,1)S(1)}, u32[]{:S(2)}, u32[]{:S(2)}) async-start(bf16[128,24,128]{2,1,0:T(8,128)(2,1)} %pad_maximum_fusion), calls=%async_computation.1 | async-start | bytes 1572864 | tf_op jit(solution)/shard_map/all_to_all | solution.py:350
  38.5 0.7 stack.33.block_ref
  39.2 0.7 pad_add_fusion.place_ref
  39.9 0.2 copy.21
  40.1 0.8 copy.20
  40.8 0.6 slice_bitcast_fusion.1
  41.5 47.9 %factor.1 = (bf16[1024,512]{1,0:T(8,128)(2,1)}, f32[1024,1]{1,0:T(8,128)}, bf16[2,3,512,512]{3,2,1,0:T(8,128)(2,1)}, bf16[512,512]{1,0:T(8,128)(2,1)}, f32[3,8,128]{2,1,0:T(8,128)}, /*index=5*/f32[3,8,128]{2,1,0:T(8,128)}) custom-call(s32[3]{0:T(128)} %pad_add_fusion.place_ref, bf16[8,128,128]{2,1,0:T(8,128)(2,1)} %bitcast.37, ...), custom_call_target="tpu_custom_call" | custom-call | tf_op jit(solution)/shard_map/factor/pallas_call | solution.py:357
  89.3 0.0 all-to-all-done.1
  89.3 1.1 copy.24
  90.4 29.9 %panel_rows.1 = (bf16[3072,128]{1,0:T(8,128)(2,1)}, f32[3072,1]{1,0:T(8,128)}, bf16[3072,1024]{1,0:T(8,128)(2,1)}) custom-call(s32[6]{0:T(128)} %stack.33.block_ref, bf16[3,8,128,128]{3,2,1,0:T(8,128)(2,1)} %bitcast.35, f32[3,8,128]{2,1,0:T(8,128)} %get-tuple-element.22.slots_ref, f32[3,8,128]{2,1,0:T(8,128)} %get-tuple-element.23.noises_ref, ...), custom_call_target="tpu_custom_call" | custom-call | tf_op jit(solution)/shard_map/panel_rows/pallas_call | solution.py:381
  120.3 15.3 %tiles.1 = bf16[1024,2048]{1,0:T(8,128)(2,1)} custom-call(s32[6]{0:T(128)} %stack.33.block_ref, bf16[3072,128]{1,0:T(8,128)(2,1)} %get-tuple-element.28.left_rows_ref.right_rows_ref, bf16[3072,128]{1,0:T(8,128)(2,1)} %get-tuple-element.28.left_rows_ref.right_rows_ref, f32[3072,1]{1,0:T(8,128)} %get-tuple-element.29.noise_ref, f32[1,128]{1,0:T(1,128)} %bitcast.44, ...), custom_call_target="tpu_custom_call" | custom-call | tf_op jit(solution)/shard_map/tiles/pallas_call | solution.py:411
  (5 shorter events, 0.1 us)
Async XLA Ops:
  4.5 13.0 %copy-start = (bf16[128,128]{1,0:T(8,128)(2,1)S(1)}, bf16[128,128]{1,0:T(8,128)(2,1)}, u32[]{:S(2)}) copy-start(bf16[128,128]{1,0:T(8,128)(2,1)} %get-tuple-element.18) | copy-start | bytes 98308
  6.9 24.1 %all-to-all-start = ((bf16[128,24,128]{2,1,0:T(8,128)(2,1)}), bf16[128,24,128]{2,1,0:T(8,128)(2,1)S(1)}, u32[]{:S(2)}, u32[]{:S(2)}) async-start(bf16[128,24,128]{2,1,0:T(8,128)(2,1)} %broadcast_in_dim.30), calls=%async_computation | async-start | bytes 1572864 | tf_op jit(solution)/shard_map/all_to_all | solution.py:342
  31.0 58.3 %all-to-all-start.1 = ((bf16[128,24,128]{2,1,0:T(8,128)(2,1)}), bf16[128,24,128]{2,1,0:T(8,128)(2,1)S(1)}, u32[]{:S(2)}, u32[]{:S(2)}) async-start(bf16[128,24,128]{2,1,0:T(8,128)(2,1)} %pad_maximum_fusion), calls=%async_computation.1 | async-start | bytes 1572864 | tf_op jit(solution)/shard_map/all_to_all | solution.py:350

commit v2 on v1

v2 whole, which is shorter than its diff:
```python
import jax
import jax.numpy as jnp
from jax import lax
from jax.experimental import pallas as pl
from jax.experimental.pallas import tpu as pltpu
from jax.sharding import PartitionSpec as P

NB = 512
PANELS = 2
F = 128
f32 = jnp.float32
bf16 = jnp.bfloat16


def split3(x):
    h = x.astype(bf16)
    r = x - h.astype(f32)
    m = r.astype(bf16)
    return h, m, (r - m.astype(f32)).astype(bf16)


def split2(x):
    h = x.astype(bf16)
    return h, (x - h.astype(f32)).astype(bf16)


def left4(pieces):
    h, m = pieces
    return jnp.concatenate([h, h, m, m], axis=1)


def right4(pieces, axis):
    h, m = pieces
    return jnp.concatenate([h, m, h, m], axis=axis)


def left3(pieces):
    h, m = pieces
    return jnp.concatenate([h, h, m], axis=1)


def right3(pieces):
    h, m = pieces
    return jnp.concatenate([h, m, h], axis=1)


def nt(x, y):
    return lax.dot_general(x, y, (((1,), (1,)), ((), ())), preferred_element_type=f32)


def nn(x, y):
    return lax.dot_general(x, y, (((1,), (0,)), ((), ())), preferred_element_type=f32)


def iota(shape, dim):
    return lax.broadcasted_iota(jnp.int32, shape, dim)


def pack_kernel(feat_ref, noise_ref, slot_ref, sorted_ref, lead_ref):
    n = feat_ref.shape[0]
    eye = iota((n, n), 0) == iota((n, n), 1)
    row = slot_ref[...].astype(f32)
    col = jnp.sum(jnp.where(eye, row, 0.0), axis=1, keepdims=True)
    noise = noise_ref[...].astype(bf16).astype(f32)
    noise = jnp.sum(jnp.where(eye, noise, 0.0), axis=1, keepdims=True)
    local = (slot_ref[...] % n).astype(f32)
    local = jnp.sum(jnp.where(eye, local, 0.0), axis=1, keepdims=True)
    rank_col = jnp.sum((row < col).astype(f32), axis=1, keepdims=True)
    rank_row = jnp.sum((col < row).astype(f32), axis=0, keepdims=True)
    pick = (iota((n, n), 0).astype(f32) == rank_row).astype(bf16)
    arranged = nn(pick, feat_ref[...].astype(bf16))
    sorted_ref[...] = arranged.astype(bf16)
    back = rank_col == iota((n, n), 1).astype(f32)
    slots = jnp.sum(jnp.where(back, local, 0.0), axis=0, keepdims=True)
    noises = jnp.sum(jnp.where(back, noise, 0.0), axis=0, keepdims=True)
    which = iota((8, n), 0)
    extra = jnp.where(which == 0, slots, jnp.where(which == 1, noises, 0.0))
    block = jnp.concatenate([arranged[:16], extra], axis=0).astype(bf16)
    lead_ref[...] = jnp.broadcast_to(block[None], lead_ref.shape)


def spread_rows(table, target):
    n = table.shape[0]
    lane = iota((n, n), 1)
    mine = jnp.where(lane // 8 == target, table, jnp.zeros_like(table))
    comb = (iota((n, n), 0) % 8 == iota((n, n), 1) % 8).astype(bf16)
    spread = nn(mine, comb).reshape(n // 8, 8, n)
    take = iota((n // 8, 8, n), 2) // 8 == iota((n // 8, 8, n), 0)
    return jnp.sum(jnp.where(take, spread, 0.0), axis=0)


def place_range(slots, noises, samples):
    n = samples.shape[0]
    hot = iota((n, n), 0).astype(f32) == slots
    rows = nn(hot.astype(bf16), samples).astype(bf16)
    noise = jnp.sum(jnp.where(hot, noises, 0.0), axis=1, keepdims=True)
    return rows, noise


def fill_lanes(values, width):
    lane = iota((values[0].shape[0], width), 1)
    out = jnp.zeros((values[0].shape[0], width), f32)
    for i, v in enumerate(values):
        out = jnp.where(lane == i, v, out)
    return out.astype(bf16)


def half_norm(x, scale):
    return -0.5 * jnp.sum(x * x * scale, axis=1, keepdims=True)


def left_operand(rows, scale):
    h, m, l = split3(half_norm(rows.astype(f32), scale))
    extra = fill_lanes([1.0 + 0.0 * h.astype(f32)] * 3 + [h.astype(f32), m.astype(f32), l.astype(f32)], F)
    return jnp.concatenate([rows, rows, rows, extra], axis=1)


def right_operand(rows, scale):
    x = rows.astype(f32)
    h, m, l = split3(half_norm(x, scale))
    extra = fill_lanes([h.astype(f32), m.astype(f32), l.astype(f32)] + [1.0 + 0.0 * h.astype(f32)] * 3, F)
    return jnp.concatenate([*split3(x * scale), extra], axis=1)


def add_diagonal(value, noise):
    n = value.shape[0]
    return value + jnp.where(iota((n, n), 0) == iota((n, n), 1), noise, 0.0)


def lane(x, j):
    return jnp.broadcast_to(x[:, j : j + 1], (8, 128))


def invert_factor(block, spill_ref):
    def sub(q, k):
        return jnp.broadcast_to(spill_ref[q, k : k + 1, :], (8, 128))

    ri = iota((8, 128), 0)
    ci = iota((8, 128), 1)
    a = [block[8 * i : 8 * i + 8, :] for i in range(16)]
    b = [(ri + 8 * i == ci).astype(f32) for i in range(16)]
    out = []
    for g in range(16):
        o = 16 * (g % 2)
        cb = [lane(a[g], 8 * g + k) for k in range(8)]
        for k in range(8):
            spill_ref[o + k] = cb[k]
        spill_ref[o + 8] = a[g]
        spill_ref[o + 9] = b[g]
        d = [[sub(o + k, r) if r >= k else None for k in range(8)] for r in range(8)]
        ar = [sub(o + 8, k) for k in range(8)]
        br = [sub(o + 9, k) for k in range(8)]
        more = g + 1 < 16
        cc = [lane(a[g + 1], 8 * g + k) for k in range(8)] if more else None
        rs = [None] * 8
        l = [[None] * 8 for _ in range(8)]
        for k in range(8):
            rs[k] = lax.rsqrt(d[k][k])
            for m in range(k + 1, 8):
                l[m][k] = d[m][k] * rs[k]
            for m in range(k + 1, 8):
                for j in range(k + 1, m + 1):
                    d[m][j] = d[m][j] - l[m][k] * l[j][k]
            ar[k] = ar[k] * rs[k]
            br[k] = br[k] * rs[k]
            if more:
                cc[k] = cc[k] * rs[k]
            for m in range(k + 1, 8):
                ar[m] = ar[m] - l[m][k] * ar[k]
                br[m] = br[m] - l[m][k] * br[k]
                if more:
                    cc[m] = cc[m] - l[m][k] * cc[k]
            if more:
                a[g + 1] = a[g + 1] - cc[k] * ar[k]
                b[g + 1] = b[g + 1] - cc[k] * br[k]
        v = br[7]
        for k in range(7):
            v = jnp.where(ri == k, br[k], v)
        out.append(v)
        if g + 2 < 16:
            z = [None] * 8
            y = [None] * 8
            for k in range(7, -1, -1):
                zz = ar[k]
                yy = br[k]
                for m in range(7, k, -1):
                    zz = zz - l[m][k] * z[m]
                    yy = yy - l[m][k] * y[m]
                z[k] = zz * rs[k]
                y[k] = yy * rs[k]
            for i in range(g + 2, 16):
                ai = a[i]
                bi = b[i]
                for k in range(8):
                    c = lane(a[i], 8 * g + k)
                    ai = ai - c * z[k]
                    bi = bi - c * y[k]
                a[i] = ai
                b[i] = bi
    return jnp.concatenate(out, axis=0)


def invert_panel(a_ref, w_ref, spill_ref):
    w_ref[...] = jnp.zeros((NB, NB), f32)
    for s in range(0, NB, 128):
        e = s + 128
        w = invert_factor(a_ref[s:e, s:e], spill_ref)
        pieces = split2(w)
        wl = left4(pieces)
        if e < NB:
            low = nt(left4(split2(a_ref[e:NB, s:e])), right4(pieces, 1))
            low_pieces = split2(low)
            low_left = left4(low_pieces)
            a_ref[e:NB, e:NB] = a_ref[e:NB, e:NB] - nt(low_left, right4(low_pieces, 1))
        if s > 0:
            w_ref[s:e, 0:s] = nn(wl, right4(split2(w_ref[s:e, 0:s]), 0))
        w_ref[s:e, s:e] = w
        if e < NB:
            w_ref[e:NB, 0:e] = w_ref[e:NB, 0:e] - nn(low_left, right4(split2(w_ref[s:e, 0:e]), 0))


def times_inverse(left, pieces):
    half = NB // 2
    lp = split2(left)
    top = nt(left3([p[:, :half] for p in lp]), right3([p[:half, :half] for p in pieces]))
    bottom = nt(left3(lp), right3([p[half:, :] for p in pieces]))
    return jnp.concatenate([top, bottom], axis=1)


def factor_kernel(
    block_ref, samples_ref, slot_ref, noise_ref, scale_ref,
    right_ref, lead_noise_ref, w_ref, p21_ref, slots_ref, noises_ref, a_ref, inv_ref, spill_ref,
):
    scale = scale_ref[...]
    slot_table = slot_ref[...]
    noise_table = noise_ref[...]
    for panel in range(PANELS):
        slots = spread_rows(slot_table, panel)
        noises = spread_rows(noise_table, panel)
        rows = []
        for i in range(4):
            placed, noise = place_range(
                slots[i : i + 1, :], noises[i : i + 1, :], samples_ref[panel * 4 + i]
            )
            rows.append(placed)
            lead_noise_ref[panel * NB + i * 128 : panel * NB + (i + 1) * 128, :] = noise
        rows = jnp.concatenate(rows, axis=0)
        right_ref[panel * NB : (panel + 1) * NB, :] = right_operand(rows, scale)
        left = left_operand(rows, scale)
        for other in range(panel + 1):
            value = jnp.exp(nt(left, right_ref[other * NB : (other + 1) * NB, :]))
            if other == panel:
                value = add_diagonal(value, lead_noise_ref[panel * NB : (panel + 1) * NB, :])
            a_ref[panel + other] = value

    for kind in range(3):
        target = block_ref[(0, 2, 3)[kind]]
        slots_ref[kind] = spread_rows(slot_table, target)
        noises_ref[kind] = spread_rows(noise_table, target)

    def one_panel(panel, carry):
        invert_panel(a_ref.at[0], inv_ref, spill_ref)
        pieces = split2(inv_ref[...])
        for i in range(2):
            w_ref[panel, i] = pieces[i]

        @pl.when(panel == 0)
        def _():
            p21 = times_inverse(a_ref[1], pieces).astype(bf16)
            p21_ref[...] = p21
            a_ref[0] = a_ref[2] - nt(p21, p21)

        return carry

    lax.fori_loop(0, PANELS, one_panel, 0)


def kind_of(step):
    step = jnp.minimum(step, 5)
    return jnp.where(step < 2, 0, 1 + step % 2), jnp.where(step < 2, step, (step - 2) // 2)


def output_kernel(
    block_ref, samples_ref, slots_ref, noises_ref, scale_ref, lead_ref, lead_noise_ref,
    w_ref, p21_ref, out_ref, p_ref, left_ref, right_ref, noise_ref, k_ref,
):
    step = pl.program_id(0)

    @pl.when(step < 6)
    def _():
        kind, half = kind_of(step)
        block = block_ref[step]
        rows = []
        for i in range(4):
            placed, noise = place_range(
                slots_ref[kind, pl.ds(4 * half + i, 1), :],
                noises_ref[kind, pl.ds(4 * half + i, 1), :],
                samples_ref[:, i].reshape(128, F),
            )
            rows.append(placed)
            noise_ref[step, i * 128 : (i + 1) * 128, :] = noise
        rows = jnp.concatenate(rows, axis=0)
        scale = scale_ref[...]
        left = left_operand(rows, scale)

        @pl.when(step < 2)
        def _():
            left_ref[step] = left

        @pl.when(step >= 2)
        def _():
            right_ref[step - 2] = right_operand(rows, scale)

        for panel in range(PANELS):
            value = jnp.exp(nt(left, lead_ref[panel * NB : (panel + 1) * NB, :]))
            k_ref[panel] = value

        @pl.when(block < PANELS)
        def _():
            k_ref[block] = add_diagonal(k_ref[block], lead_noise_ref[pl.ds(block * NB, NB), :])

        p1 = times_inverse(k_ref[0], [w_ref[0, i] for i in range(2)]).astype(bf16)
        second = k_ref[1] - nt(p1, p21_ref[...])
        p2 = times_inverse(second, [w_ref[1, i] for i in range(2)]).astype(bf16)
        p_ref[step, :, :NB] = p1
        p_ref[step, :, NB:] = jnp.where(block >= 1, p2, jnp.zeros_like(p2))

    @pl.when(step >= 6)
    def _():
        i = (step - 6) % 2
        j = (step - 6) // 2
        row_block = block_ref[i]
        col_block = block_ref[2 + j]

        @pl.when(col_block == 0)
        def _():
            out_ref[...] = p_ref[i, :, :NB]

        @pl.when(col_block == 1)
        def _():
            out_ref[...] = p_ref[i, :, NB:]

        @pl.when((col_block >= PANELS) & (row_block < PANELS))
        def _():
            out_ref[...] = jnp.zeros(out_ref.shape, bf16)

        @pl.when((col_block >= PANELS) & (row_block >= PANELS))
        def _():
            value = jnp.exp(nt(left_ref[i], right_ref[j])) - nt(p_ref[i], p_ref[2 + j])

            @pl.when(row_block != col_block)
            def _():
                out_ref[...] = value.astype(bf16)

            @pl.when(row_block == col_block)
            def _():
                out_ref[...] = add_diagonal(value, noise_ref[i]).astype(bf16)


VMEM = pl.BlockSpec(memory_space=pltpu.VMEM)
SMEM = pl.BlockSpec(memory_space=pltpu.SMEM)
PARAMS = pltpu.CompilerParams(vmem_limit_bytes=56 * 1024 * 1024)


def body(features, noise, owner_slot, inv_length):
    nrows = lax.axis_size("row")
    ncols = lax.axis_size("col")
    here = features.shape[0]
    count = nrows * ncols
    r = lax.axis_index("row").astype(jnp.int32)
    c = lax.axis_index("col").astype(jnp.int32)
    scale = inv_length.reshape(1, F)

    arranged, lead_send = pl.pallas_call(
        pack_kernel,
        out_shape=(
            jax.ShapeDtypeStruct((here, F), bf16),
            jax.ShapeDtypeStruct((count, 24, F), bf16),
        ),
        in_specs=[VMEM] * 3,
        out_specs=(VMEM, VMEM),
        name="pack",
    )(features, noise.reshape(1, here), owner_slot.reshape(1, here))
    lead = lax.all_to_all(lead_send, ("row", "col"), 0, 0, tiled=True)

    groups = arranged.reshape(nrows, 8, F)
    to_row = jnp.broadcast_to(groups[:, None], (nrows, ncols, 8, F))
    to_col = jnp.broadcast_to(groups.reshape(1, 2, ncols, 8, F), (nrows, 2, ncols, 8, F))
    bulk_send = jnp.concatenate([to_row, to_col[:, 0], to_col[:, 1]], axis=2)
    bulk_send = bulk_send.reshape(count, 24, F)
    bulk_send, lead = lax.optimization_barrier((bulk_send, lead))
    bulk = lax.all_to_all(bulk_send, ("row", "col"), 0, 0, tiled=True)

    lead_samples = lead.reshape(nrows, ncols, 24, F)[:, :4, :16].reshape(nrows, 4, 2, 8, F)
    lead_samples = lead_samples.transpose(2, 1, 0, 3, 4).reshape(8, here, F)
    blocks = jnp.stack([r, r + nrows, c, c + ncols, c + 2 * ncols, c + 3 * ncols])

    right, lead_noise, w, p21, slots, noises = pl.pallas_call(
        factor_kernel,
        out_shape=(
            jax.ShapeDtypeStruct((PANELS * NB, 4 * F), bf16),
            jax.ShapeDtypeStruct((PANELS * NB, 1), f32),
            jax.ShapeDtypeStruct((PANELS, 2, NB, NB), bf16),
            jax.ShapeDtypeStruct((NB, NB), bf16),
            jax.ShapeDtypeStruct((3, 8, here), f32),
            jax.ShapeDtypeStruct((3, 8, here), f32),
        ),
        in_specs=[SMEM] + [VMEM] * 4,
        out_specs=(VMEM,) * 6,
        scratch_shapes=[
            pltpu.VMEM((3, NB, NB), f32),
            pltpu.VMEM((NB, NB), f32),
            pltpu.VMEM((32, 8, 128), f32),
        ],
        compiler_params=PARAMS,
        name="factor",
    )(blocks, lead_samples, lead[:, 16], lead[:, 17], scale)

    whole = lambda *shape: pl.BlockSpec(shape, lambda i, b: (0,) * len(shape))

    def samples_of(i, b):
        kind, half = kind_of(i)
        return 0, half, kind, 0

    def tile_of(i, b):
        tile = jnp.maximum(i - 6, 0)
        return tile % 2, tile // 2

    return pl.pallas_call(
        output_kernel,
        grid_spec=pltpu.PrefetchScalarGridSpec(
            num_scalar_prefetch=1,
            grid=(14,),
            in_specs=[
                pl.BlockSpec((nrows, 4, 8, F), samples_of),
                whole(3, 8, here),
                whole(3, 8, here),
                whole(1, F),
                whole(PANELS * NB, 4 * F),
                whole(PANELS * NB, 1),
                whole(PANELS, 2, NB, NB),
                whole(NB, NB),
            ],
            out_specs=pl.BlockSpec((NB, NB), tile_of),
            scratch_shapes=[
                pltpu.VMEM((6, NB, PANELS * NB), bf16),
                pltpu.VMEM((2, NB, 4 * F), bf16),
                pltpu.VMEM((4, NB, 4 * F), bf16),
                pltpu.VMEM((6, NB, 1), f32),
                pltpu.VMEM((PANELS, NB, NB), f32),
            ],
        ),
        out_shape=jax.ShapeDtypeStruct((2 * NB, 4 * NB), bf16),
        compiler_params=PARAMS,
        name="output",
    )(
        blocks, bulk.reshape(nrows, ncols, 24, F), slots, noises, scale, right, lead_noise, w, p21
    )


def solution(mesh):
    in_specs = (P(("row", "col"), None), P(("row", "col")), P(("row", "col")), P())
    out_specs = P("row", "col")
    return jax.shard_map(body, mesh=mesh, in_specs=in_specs, out_specs=out_specs, check_vma=False)
```

time: 136 us -> 108 us (0.79)
  Pallas kernels: 94.7 us -> 73.2 us
  local copies, waits for them, and re-layouts: 7.98 us -> 3.19 us
    pallas_call x1, Pallas kernels: 47.9 us -> 35.2 us  [body(): pl.pallas_call(factor_kernel, out_shape=(jax.ShapeDtypeStruct((PANELS * N...]
    pallas_call x2 -> x1, Pallas kernels: 45.2 us -> 36 us  [body(): pl.pallas_call(output_kernel, grid_spec=pltpu.PrefetchScalarGridSpec(num_...]
    reshape x2 -> x0, local copies, waits for them, and re-layouts: 2.77 us -> none  [the longest x1 1.39 us: body(): noise.reshape(here, 1)]
  transfers between devices with their start and end apart: 2 -> 2, of which waited for: 1 -> 1; matrix products, arithmetic and copies ran while one was open for 3% -> 3% of each run, Pallas kernels for 35% -> 33%
where the time goes in v2:
time: 108 us
  Pallas kernels  73.2 us (68%)
  starting transfers between devices  18.2 us (17%)
  waiting for transfers between devices  12.2 us (11%)
  local copies, waits for them, and re-layouts  3.19 us (3%)
    pallas_call x1, Pallas kernels, body(): pl.pallas_call(output_kernel, grid_spec=pltpu.PrefetchScalarGridSpec(num_...  36 us
    pallas_call x1, Pallas kernels, body(): pl.pallas_call(factor_kernel, out_shape=(jax.ShapeDtypeStruct((PANELS * N...  35.2 us
    all_to_all x1, waiting for transfers between devices, body(): lead = lax.all_to_all(lead_send, ('row', 'col'), 0, 0, tiled=True)  12.2 us
    all_to_all x1, starting transfers between devices, body(): lead = lax.all_to_all(lead_send, ('row', 'col'), 0, 0, tiled=True)  10.6 us
    all_to_all x1, starting transfers between devices, body(): bulk = lax.all_to_all(bulk_send, ('row', 'col'), 0, 0, tiled=True)  7.53 us
  transfers between devices with their start and end apart: 2, of which 1 were waited for; matrix products, arithmetic and copies ran while one was open for 3% of the time, Pallas kernels for 33%

profile of v2, /device:TPU:19, one launch (start us, length us, event | category | flops | bytes accessed | tf_op | source)
XLA Modules:
  0.0 107.9 jit_solution(2428466247704204941)
XLA Ops:
  0.0 2.0 %pack.1 = (bf16[128,128]{1,0:T(8,128)(2,1)}, bf16[128,24,128]{2,1,0:T(8,128)(2,1)}) custom-call(f32[128,128]{1,0:T(8,128)} %feat_ref.1, f32[1,128]{1,0:T(1,128)} %bitcast.37, s32[1,128]{1,0:T(1,128)} %bitcast.38), custom_call_target="tpu_custom_call" | custom-call | tf_op jit(solution)/shard_map/pack/pallas_call | solution.py:374
  2.0 0.0 copy-start.1
  2.0 10.6 %all-to-all-start = ((bf16[128,24,128]{2,1,0:T(8,128)(2,1)}), bf16[128,24,128]{2,1,0:T(8,128)(2,1)S(1)}, u32[]{:S(2)}, u32[]{:S(2)}) async-start(bf16[128,24,128]{2,1,0:T(8,128)(2,1)} %get-tuple-element.16), calls=%async_computation | async-start | bytes 1572864 | tf_op jit(solution)/shard_map/all_to_all | solution.py:384
  12.6 0.0 copy-done.1
  12.8 1.0 pad_maximum_fusion
  13.8 12.2 %all-to-all-done = bf16[128,24,128]{2,1,0:T(8,128)(2,1)S(1)} async-done(((bf16[128,24,128]{2,1,0:T(8,128)(2,1)}), bf16[128,24,128]{2,1,0:T(8,128)(2,1)S(1)}, u32[]{:S(2)}, u32[]{:S(2)}) %all-to-all-start) | async-done | bytes 786464 | tf_op jit(solution)/shard_map/all_to_all | solution.py:384
  26.1 7.5 %all-to-all-start.1 = ((bf16[128,24,128]{2,1,0:T(8,128)(2,1)}), bf16[128,24,128]{2,1,0:T(8,128)(2,1)S(1)}, u32[]{:S(2)}, u32[]{:S(2)}) async-start(bf16[128,24,128]{2,1,0:T(8,128)(2,1)} %pad_maximum_fusion), calls=%async_computation.1 | async-start | bytes 1572864 | tf_op jit(solution)/shard_map/all_to_all | solution.py:392
  33.6 0.6 stack.27.block_ref
  34.3 0.2 copy.10
  34.4 0.8 copy.9
  35.2 0.6 slice_bitcast_fusion.1
  35.8 35.2 %factor.1 = (bf16[1024,512]{1,0:T(8,128)(2,1)}, f32[1024,1]{1,0:T(8,128)}, bf16[2,2,512,512]{3,2,1,0:T(8,128)(2,1)}, bf16[512,512]{1,0:T(8,128)(2,1)}, f32[3,8,128]{2,1,0:T(8,128)}, /*index=5*/f32[3,8,128]{2,1,0:T(8,128)}) custom-call(s32[6]{0:T(128)} %stack.27.block_ref, bf16[8,128,128]{2,1,0:T(8,128)(2,1)} %bitcast.30, ...), custom_call_target="tpu_custom_call" | custom-call | tf_op jit(solution)/shard_map/factor/pallas_call | solution.py:398
  71.0 0.0 all-to-all-done.1
  71.0 0.0 copy-start
  71.0 0.9 copy-done
  71.9 36.0 %output.1 = bf16[1024,2048]{1,0:T(8,128)(2,1)} custom-call(s32[6]{0:T(128)} %stack.27.block_ref, bf16[16,8,24,128]{3,2,1,0:T(8,128)(2,1)} %bitcast.29, f32[3,8,128]{2,1,0:T(8,128)} %get-tuple-element.19.slots_ref, f32[3,8,128]{2,1,0:T(8,128)} %get-tuple-element.20.noises_ref, f32[1,128]{1,0:T(1,128)} %bitcast.36, ...), custom_call_target="tpu_custom_call" | custom-call | tf_op jit(solution)/shard_map/output/pallas_call | solution.py:429
  (5 shorter events, 0.1 us)
Async XLA Ops:
  2.0 10.6 %copy-start.1 = (bf16[128,128]{1,0:T(8,128)(2,1)S(1)}, bf16[128,128]{1,0:T(8,128)(2,1)}, u32[]{:S(2)}) copy-start(bf16[128,128]{1,0:T(8,128)(2,1)} %get-tuple-element.15) | copy-start | bytes 98308
  2.0 24.1 %all-to-all-start = ((bf16[128,24,128]{2,1,0:T(8,128)(2,1)}), bf16[128,24,128]{2,1,0:T(8,128)(2,1)S(1)}, u32[]{:S(2)}, u32[]{:S(2)}) async-start(bf16[128,24,128]{2,1,0:T(8,128)(2,1)} %get-tuple-element.16), calls=%async_computation | async-start | bytes 1572864 | tf_op jit(solution)/shard_map/all_to_all | solution.py:384
  26.1 44.9 %all-to-all-start.1 = ((bf16[128,24,128]{2,1,0:T(8,128)(2,1)}), bf16[128,24,128]{2,1,0:T(8,128)(2,1)S(1)}, u32[]{:S(2)}, u32[]{:S(2)}) async-start(bf16[128,24,128]{2,1,0:T(8,128)(2,1)} %pad_maximum_fusion), calls=%async_computation.1 | async-start | bytes 1572864 | tf_op jit(solution)/shard_map/all_to_all | solution.py:392
  71.0 0.9 copy-start

commit v3 on v2

v3 whole, which is shorter than its diff:
```python
import jax
import jax.numpy as jnp
from jax import lax
from jax.experimental import pallas as pl
from jax.experimental.pallas import tpu as pltpu
from jax.sharding import PartitionSpec as P

NB = 512
PANELS = 2
F = 128
f32 = jnp.float32
bf16 = jnp.bfloat16


def split2(x):
    h = x.astype(bf16)
    return h, (x - h.astype(f32)).astype(bf16)


def left4(pieces):
    h, m = pieces
    return jnp.concatenate([h, h, m, m], axis=1)


def right4(pieces, axis):
    h, m = pieces
    return jnp.concatenate([h, m, h, m], axis=axis)


def left3(pieces):
    h, m = pieces
    return jnp.concatenate([h, h, m], axis=1)


def right3(pieces):
    h, m = pieces
    return jnp.concatenate([h, m, h], axis=1)


def nt(x, y):
    return lax.dot_general(x, y, (((1,), (1,)), ((), ())), preferred_element_type=f32)


def nn(x, y):
    return lax.dot_general(x, y, (((1,), (0,)), ((), ())), preferred_element_type=f32)


def iota(shape, dim):
    return lax.broadcasted_iota(jnp.int32, shape, dim)


def pack_kernel(feat_ref, noise_ref, slot_ref, sorted_ref, lead_ref):
    n = feat_ref.shape[0]
    eye = iota((n, n), 0) == iota((n, n), 1)
    row = slot_ref[...].astype(f32)
    col = jnp.sum(jnp.where(eye, row, 0.0), axis=1, keepdims=True)
    noise = noise_ref[...].astype(bf16).astype(f32)
    noise = jnp.sum(jnp.where(eye, noise, 0.0), axis=1, keepdims=True)
    local = (slot_ref[...] % n).astype(f32)
    local = jnp.sum(jnp.where(eye, local, 0.0), axis=1, keepdims=True)
    rank_col = jnp.sum((row < col).astype(f32), axis=1, keepdims=True)
    rank_row = jnp.sum((col < row).astype(f32), axis=0, keepdims=True)
    arranged = nn((iota((n, n), 0).astype(f32) == rank_row).astype(bf16), feat_ref[...].astype(bf16))
    sorted_ref[...] = arranged.astype(bf16)
    back = rank_col == iota((n, n), 1).astype(f32)
    slots = jnp.sum(jnp.where(back, local, 0.0), axis=0, keepdims=True)
    noises = jnp.sum(jnp.where(back, noise, 0.0), axis=0, keepdims=True)
    c = lax.axis_index("col").astype(jnp.int32)
    which = iota((8, n), 0)
    extra = jnp.where(which == c, slots, jnp.where((which + 4) % 8 == c, noises, 0.0))
    block = jnp.concatenate([arranged[:16], extra], axis=0).astype(bf16)
    lead_ref[...] = jnp.broadcast_to(block[None], lead_ref.shape)


def spread_rows(table, target):
    n = table.shape[0]
    lane = iota((n, n), 1)
    mine = jnp.where(lane // 8 == target, table, jnp.zeros_like(table))
    comb = (iota((n, n), 0) % 8 == iota((n, n), 1) % 8).astype(bf16)
    spread = nn(mine, comb).reshape(n // 8, 8, n)
    take = iota((n // 8, 8, n), 2) // 8 == iota((n // 8, 8, n), 0)
    return jnp.sum(jnp.where(take, spread, 0.0), axis=0)


def read_tables(lead_ref):
    nrows = lead_ref.shape[0]
    slots, noises = [], []
    low = iota((8, 128), 0) < 4
    for r in range(nrows):
        parts = [lead_ref[r, c, 16:24, :].astype(f32) for c in range(8)]
        first = (parts[0] + parts[1]) + (parts[2] + parts[3])
        last = (parts[4] + parts[5]) + (parts[6] + parts[7])
        slots.append(jnp.where(low, first, last))
        other = jnp.where(low, last, first)
        noises.append(jnp.concatenate([other[4:], other[:4]], axis=0))
    return (
        jnp.concatenate(slots, axis=0).astype(bf16),
        jnp.concatenate(noises, axis=0).astype(bf16),
    )


def positions():
    nrows = lax.axis_size("row")
    ncols = lax.axis_size("col")
    r = lax.axis_index("row").astype(jnp.int32)
    c = lax.axis_index("col").astype(jnp.int32)
    return [r, r + nrows, c, c + 2 * ncols, c + ncols, c + 3 * ncols]


def pick(values, index):
    out = values[0]
    for i, v in enumerate(values[1:]):
        out = jnp.where(index == i + 1, v, out)
    return out


def one_hot(slots):
    n = slots.shape[1]
    return (iota((n, n), 0).astype(f32) == slots).astype(bf16)


def place_noise(hot, noises):
    return nt(hot, jnp.broadcast_to(noises.astype(bf16), hot.shape))


def norm_pieces(rows, scale):
    x = rows.astype(f32)
    return jnp.concatenate(split2(-0.5 * (x * x * scale)), axis=1)


def left_operand(rows, scale):
    norm = nn(norm_pieces(rows, scale), jnp.ones((2 * F, 128), bf16))
    return jnp.concatenate([rows, rows], axis=1), norm


def right_operand(rows, scale):
    norm = nt(jnp.ones((8, 2 * F), bf16), norm_pieces(rows, scale))
    return jnp.concatenate(split2(rows.astype(f32) * scale), axis=1), norm


def kernel_values(left, left_norm, right, right_norm):
    wide = jnp.concatenate([left_norm] * (right.shape[0] // 128), axis=1)
    return jnp.exp(nt(left, right) + wide + right_norm[0:1, :])


def add_diagonal(value, noise, start=0):
    n, width = value.shape
    eye = iota((128, 128), 0) == iota((128, 128), 1)
    bands = []
    for i in range(0, n, 128):
        band = value[i : i + 128, :]
        at = start + i
        square = band[:, at : at + 128] + jnp.where(eye, noise[i : i + 128, :], 0.0)
        parts = [band[:, :at], square, band[:, at + 128 :]]
        bands.append(jnp.concatenate([p for p in parts if p.shape[1]], axis=1))
    return jnp.concatenate(bands, axis=0)


def lane(x, j):
    return jnp.broadcast_to(x[:, j : j + 1], (8, 128))


def invert_factor(block, spill_ref, filler=None):
    def sub(q, k):
        return jnp.broadcast_to(spill_ref[q, k : k + 1, :], (8, 128))

    ri = iota((8, 128), 0)
    ci = iota((8, 128), 1)
    a = [block[8 * i : 8 * i + 8, :] for i in range(16)]
    b = [(ri + 8 * i == ci).astype(f32) for i in range(16)]
    out = []
    held = None
    for g in range(16):
        even = g % 2 == 0
        o = 32 * (g % 2)
        cb = [lane(a[g], 8 * g + k) for k in range(8)] if even else held
        cc = [lane(a[g + 1], 8 * g + k) for k in range(8)] if even else None
        nb = [lane(a[g + 1], 8 * g + 8 + k) for k in range(8)] if even else None
        for k in range(8):
            spill_ref[o + k] = cb[k]
        spill_ref[o + 8] = a[g]
        spill_ref[o + 9] = b[g]
        d = [[sub(o + k, r) if r >= k else None for k in range(8)] for r in range(8)]
        ar = [sub(o + 8, k) for k in range(8)]
        br = [sub(o + 9, k) for k in range(8)]
        rs = [None] * 8
        l = [[None] * 8 for _ in range(8)]

        def apply(k):
            ar[k] = ar[k] * rs[k]
            br[k] = br[k] * rs[k]
            if even:
                cc[k] = cc[k] * rs[k]
            for m in range(k + 1, 8):
                ar[m] = ar[m] - l[m][k] * ar[k]
                br[m] = br[m] - l[m][k] * br[k]
                if even:
                    cc[m] = cc[m] - l[m][k] * cc[k]
            if even:
                a[g + 1] = a[g + 1] - cc[k] * ar[k]
                b[g + 1] = b[g + 1] - cc[k] * br[k]
                spill_ref[o + 16 + k] = cc[k]
                for q in range(8):
                    nb[q] = nb[q] - cc[k] * sub(o + 16 + k, q)

        for k in range(0, 8, 2):
            r0 = lax.rsqrt(d[k][k])
            det = d[k][k] * d[k + 1][k + 1] - d[k + 1][k] * d[k + 1][k]
            rs[k] = r0
            rs[k + 1] = lax.rsqrt(det) * (d[k][k] * r0)
            for m in range(k + 1, 8):
                l[m][k] = d[m][k] * r0
            for m in range(k + 2, 8):
                l[m][k + 1] = (d[m][k + 1] - l[m][k] * l[k + 1][k]) * rs[k + 1]
            for m in range(k + 2, 8):
                for j in range(k + 2, m + 1):
                    d[m][j] = (d[m][j] - l[m][k] * l[j][k]) - l[m][k + 1] * l[j][k + 1]
            apply(k)
            apply(k + 1)
        if even:
            held = nb
        v = br[7]
        for k in range(7):
            v = jnp.where(ri == k, br[k], v)
        out.append(v)
        if filler is not None:
            next(filler, None)
        first = g + 2 if even else g + 1
        if first < 16:
            z = [None] * 8
            y = [None] * 8
            for k in range(7, -1, -1):
                zz = ar[k]
                yy = br[k]
                for m in range(7, k, -1):
                    zz = zz - l[m][k] * z[m]
                    yy = yy - l[m][k] * y[m]
                z[k] = zz * rs[k]
                y[k] = yy * rs[k]
            for i in range(first, 16):
                ai = a[i]
                bi = b[i]
                for k in range(8):
                    c = lane(a[i], 8 * g + k)
                    ai = ai - c * z[k]
                    bi = bi - c * y[k]
                a[i] = ai
                b[i] = bi
    return jnp.concatenate(out, axis=0)


def invert_panel(a_ref, w_ref, spill_ref, fillers=(None,) * 4):
    w_ref[...] = jnp.zeros((NB, NB), f32)
    for s in range(0, NB, 128):
        e = s + 128
        filler = fillers[s // 128]
        w = invert_factor(a_ref[s:e, s:e], spill_ref, filler)
        if filler is not None:
            for _ in filler:
                pass
        pieces = split2(w)
        wl = left4(pieces)
        if e < NB:
            low = nt(left4(split2(a_ref[e:NB, s:e])), right4(pieces, 1))
            low_pieces = split2(low)
            low_left = left4(low_pieces)
            a_ref[e:NB, e:NB] = a_ref[e:NB, e:NB] - nt(low_left, right4(low_pieces, 1))
        if s > 0:
            w_ref[s:e, 0:s] = nn(wl, right4(split2(w_ref[s:e, 0:s]), 0))
        w_ref[s:e, s:e] = w
        if e < NB:
            w_ref[e:NB, 0:e] = w_ref[e:NB, 0:e] - nn(low_left, right4(split2(w_ref[s:e, 0:e]), 0))


def times_inverse(left, pieces):
    half = NB // 2
    lp = split2(left)
    top = nt(left3([p[:, :half] for p in lp]), right3([p[:half, :half] for p in pieces]))
    bottom = nt(left3(lp), right3([p[half:, :] for p in pieces]))
    return jnp.concatenate([top, bottom], axis=1)


def factor_kernel(
    lead_ref, scale_ref,
    right_ref, norm_ref, lead_noise_ref, w_ref, p21_ref, slots_ref, noises_ref, next_ref,
    a_ref, inv_ref, spill_ref,
):
    scale = scale_ref[...]
    slot_table, noise_table = read_tables(lead_ref)

    def lead_rows(panel):
        slots = spread_rows(slot_table, panel)
        noises = spread_rows(noise_table, panel)
        rows = []
        for c in range(4):
            hot = one_hot(slots[c : c + 1, :])
            at = panel * NB + c * 128
            rows.append(nn(hot, lead_ref[:, c, 8 * panel : 8 * panel + 8, :].reshape(128, F)))
            lead_noise_ref[at : at + 128, :] = place_noise(hot, noises[c : c + 1, :])
        rows = jnp.concatenate(rows, axis=0).astype(bf16)
        right_ref[panel], norm_ref[panel] = right_operand(rows, scale)
        return left_operand(rows, scale)

    a_ref[0] = add_diagonal(
        kernel_values(*lead_rows(0), right_ref[0], norm_ref[0]), lead_noise_ref[:NB, :]
    )

    def rest():
        left = lead_rows(1)
        yield
        a_ref[1] = kernel_values(*left, right_ref[0], norm_ref[0])
        yield
        a_ref[2] = add_diagonal(
            kernel_values(*left, right_ref[1], norm_ref[1]), lead_noise_ref[NB:, :]
        )
        yield
        blocks = positions()
        for kind in range(3):
            slots_ref[kind] = spread_rows(slot_table, blocks[2 * kind])
            noises_ref[kind] = spread_rows(noise_table, blocks[2 * kind])
            yield

    invert_panel(a_ref.at[0], inv_ref, spill_ref, (rest(), None, None, None))
    pieces = split2(inv_ref[...])
    for i in range(2):
        w_ref[i] = pieces[i]
    p21 = times_inverse(a_ref[1], pieces).astype(bf16)
    p21_ref[...] = p21
    next_ref[...] = a_ref[2] - nt(p21, p21)


UNIT = 256


def second_kernel(
    bulk_ref, slots_ref, noises_ref, scale_ref, right_ref, norm_ref, lead_noise_ref,
    w_ref, next_ref, rows_ref, row_noise_ref, p1_ref, w2_ref, a_ref, inv_ref, spill_ref,
):
    a_ref[...] = next_ref[...]
    scale = scale_ref[...]
    half = NB // 2
    blocks = positions()

    def unit(index):
        block = blocks[index // 2]
        at = slice(index * UNIT, (index + 1) * UNIT)
        rows = []
        for i in range(2):
            kind, c = divmod(index * 2 + i, 8)
            hot = one_hot(slots_ref[kind, c : c + 1, :])
            rows.append(nn(hot, bulk_ref[:, c, 8 * kind : 8 * kind + 8, :].reshape(128, F)))
            if kind == 0:
                row_noise_ref[c * 128 : c * 128 + 128, :] = place_noise(
                    hot, noises_ref[kind, c : c + 1, :]
                )
        rows = jnp.concatenate(rows, axis=0).astype(bf16)
        rows_ref[at, :] = rows
        yield
        value = kernel_values(*left_operand(rows, scale), right_ref[0], norm_ref[0])
        lo = index % 2 * UNIT
        lead = jnp.where(block == 0, lead_noise_ref[lo : lo + UNIT, :], 0.0)
        pieces = split2(add_diagonal(value, lead, lo))
        yield
        top = nt(
            left3([p[:, :half] for p in pieces]),
            right3([w_ref[i, :half, :half] for i in range(2)]),
        )
        p1_ref[at, :half] = top.astype(bf16)
        yield
        bottom = nt(left3(pieces), right3([w_ref[i, half:, :] for i in range(2)]))
        p1_ref[at, half:] = bottom.astype(bf16)
        yield

    def units(first, last):
        for index in range(first, last):
            yield from unit(index)

    invert_panel(a_ref, inv_ref, spill_ref, [units(3 * i, 3 * i + 3) for i in range(4)])
    pieces = split2(inv_ref[...])
    for i in range(2):
        w2_ref[i] = pieces[i]


def output_kernel(
    rows_ref, row_noise_ref, scale_ref, lead_ref, lead_norm_ref, lead_noise_ref,
    p1_ref, p21_ref, w_ref, out_ref, p_ref, left_ref, left_norm_ref, right_ref, right_norm_ref,
):
    step = pl.program_id(0)
    blocks = positions()
    tall = 2 * NB

    @pl.when(step < 3)
    def _():
        pair = [pick(blocks[i::2], step) for i in range(2)]
        rows = rows_ref[...]
        scale = scale_ref[...]
        left, left_norm = left_operand(rows, scale)

        @pl.when(step == 0)
        def _():
            left_ref[...] = left
            left_norm_ref[...] = left_norm

        @pl.when(step >= 1)
        def _():
            right, norm = right_operand(rows, scale)
            for i in range(2):
                right_ref[2 * step - 2 + i] = right[i * NB : (i + 1) * NB, :]
                right_norm_ref[2 * step - 2 + i] = norm[:, i * NB : (i + 1) * NB]

        value = kernel_values(left, left_norm, lead_ref[1], lead_norm_ref[1])
        noise = lead_noise_ref[NB:, :]
        value = jnp.concatenate(
            [
                add_diagonal(value[i * NB : (i + 1) * NB, :], jnp.where(pair[i] == 1, noise, 0.0))
                for i in range(2)
            ],
            axis=0,
        )
        p1 = p1_ref[...]
        second = value - nt(p1, p21_ref[...])
        p2 = times_inverse(second, [w_ref[i] for i in range(2)])
        at = pl.multiple_of(step * tall, tall)
        p_ref[pl.ds(at, tall), :NB] = p1
        for i in range(2):
            kept = jnp.where(pair[i] >= 1, p2[i * NB : (i + 1) * NB, :], 0.0)
            p_ref[pl.ds(at + i * NB, NB), NB:] = kept.astype(bf16)

    @pl.when(step >= 3)
    def _():
        column = step - 3
        j = 2 * (column % 2) + column // 2
        col_block = pick(blocks[2:], j)

        @pl.when(col_block == 0)
        def _():
            out_ref[...] = p_ref[:tall, :NB]

        @pl.when(col_block == 1)
        def _():
            out_ref[...] = p_ref[:tall, NB:]

        @pl.when(col_block >= PANELS)
        def _():
            value = kernel_values(left_ref[...], left_norm_ref[...], right_ref[j], right_norm_ref[j])
            at = pl.multiple_of((2 + j) * NB, NB)
            value = value - nt(p_ref[:tall, :], p_ref[pl.ds(at, NB), :])
            for i in range(2):
                noise = row_noise_ref[i * NB : (i + 1) * NB, :]
                noise = jnp.where(blocks[i] == col_block, noise, 0.0)
                half = add_diagonal(value[i * NB : (i + 1) * NB, :], noise)
                half = jnp.where(blocks[i] >= PANELS, half, 0.0)
                out_ref[i * NB : (i + 1) * NB, :] = half.astype(bf16)


VMEM = pl.BlockSpec(memory_space=pltpu.VMEM)
SMEM = pl.BlockSpec(memory_space=pltpu.SMEM)
PARAMS = pltpu.CompilerParams(vmem_limit_bytes=56 * 1024 * 1024)


def body(features, noise, owner_slot, inv_length):
    nrows = lax.axis_size("row")
    ncols = lax.axis_size("col")
    here = features.shape[0]
    count = nrows * ncols
    scale = inv_length.reshape(1, F)

    arranged, lead_send = pl.pallas_call(
        pack_kernel,
        out_shape=(
            jax.ShapeDtypeStruct((here, F), bf16),
            jax.ShapeDtypeStruct((count, 24, F), bf16),
        ),
        in_specs=[VMEM] * 3,
        out_specs=(VMEM, VMEM),
        name="pack",
    )(features, noise.reshape(1, here), owner_slot.reshape(1, here))
    lead = lax.all_to_all(lead_send, ("row", "col"), 0, 0, tiled=True)

    groups = arranged.reshape(nrows, 8, F)
    to_row = jnp.broadcast_to(groups[:, None], (nrows, ncols, 8, F))
    to_col = jnp.broadcast_to(groups.reshape(1, 2, ncols, 8, F), (nrows, 2, ncols, 8, F))
    bulk_send = jnp.concatenate([to_row, to_col[:, 0], to_col[:, 1]], axis=2)
    bulk_send = bulk_send.reshape(count, 24, F)
    bulk_send, lead = lax.optimization_barrier((bulk_send, lead))
    bulk = lax.all_to_all(bulk_send, ("row", "col"), 0, 0, tiled=True)

    right, norm, lead_noise, w1, p21, slots, noises, trailing = pl.pallas_call(
        factor_kernel,
        out_shape=(
            jax.ShapeDtypeStruct((PANELS, NB, 2 * F), bf16),
            jax.ShapeDtypeStruct((PANELS, 8, NB), f32),
            jax.ShapeDtypeStruct((PANELS * NB, 128), f32),
            jax.ShapeDtypeStruct((2, NB, NB), bf16),
            jax.ShapeDtypeStruct((NB, NB), bf16),
            jax.ShapeDtypeStruct((3, 8, here), f32),
            jax.ShapeDtypeStruct((3, 8, here), f32),
            jax.ShapeDtypeStruct((NB, NB), f32),
        ),
        in_specs=[VMEM] * 2,
        out_specs=(VMEM,) * 8,
        scratch_shapes=[
            pltpu.VMEM((3, NB, NB), f32),
            pltpu.VMEM((NB, NB), f32),
            pltpu.VMEM((64, 8, 128), f32),
        ],
        compiler_params=PARAMS,
        name="first_panel",
    )(lead.reshape(nrows, ncols, 24, F), scale)

    rows, row_noise, p1, w2 = pl.pallas_call(
        second_kernel,
        out_shape=(
            jax.ShapeDtypeStruct((6 * NB, F), bf16),
            jax.ShapeDtypeStruct((2 * NB, 128), f32),
            jax.ShapeDtypeStruct((6 * NB, NB), bf16),
            jax.ShapeDtypeStruct((2, NB, NB), bf16),
        ),
        in_specs=[VMEM] * 9,
        out_specs=(VMEM,) * 4,
        scratch_shapes=[
            pltpu.VMEM((NB, NB), f32),
            pltpu.VMEM((NB, NB), f32),
            pltpu.VMEM((64, 8, 128), f32),
        ],
        compiler_params=PARAMS,
        name="second_panel",
    )(
        bulk.reshape(nrows, ncols, 24, F), slots, noises, scale, right, norm, lead_noise, w1,
        trailing,
    )

    whole = lambda *shape: pl.BlockSpec(shape, lambda i: (0,) * len(shape))
    tall = lambda *shape: pl.BlockSpec(shape, lambda i: (jnp.minimum(i, 2), 0))
    return pl.pallas_call(
        output_kernel,
        grid=(7,),
        in_specs=[
            tall(2 * NB, F),
            whole(2 * NB, 128),
            whole(1, F),
            whole(PANELS, NB, 2 * F),
            whole(PANELS, 8, NB),
            whole(PANELS * NB, 128),
            tall(2 * NB, NB),
            whole(NB, NB),
            whole(2, NB, NB),
        ],
        out_specs=pl.BlockSpec((2 * NB, NB), lambda i: (0, jnp.maximum(i - 3, 0))),
        scratch_shapes=[
            pltpu.VMEM((6 * NB, PANELS * NB), bf16),
            pltpu.VMEM((2 * NB, 2 * F), bf16),
            pltpu.VMEM((2 * NB, 128), f32),
            pltpu.VMEM((4, NB, 2 * F), bf16),
            pltpu.VMEM((4, 8, NB), f32),
        ],
        out_shape=jax.ShapeDtypeStruct((2 * NB, 4 * NB), bf16),
        compiler_params=PARAMS,
        name="output",
    )(rows, row_noise, scale, right, norm, lead_noise, p1, p21, w2)


def solution(mesh):
    in_specs = (P(("row", "col"), None), P(("row", "col")), P(("row", "col")), P())
    out_specs = P("row", "col")
    return jax.shard_map(body, mesh=mesh, in_specs=in_specs, out_specs=out_specs, check_vma=False)
```

time: 108 us -> 92 us (0.85)
  Pallas kernels: 73.2 us -> 58.9 us
  local copies, waits for them, and re-layouts: 3.19 us -> 1.03 us
    pallas_call x2 -> x3, Pallas kernels: 71.2 us -> 56.9 us  [the longest x1 20 us: body(): pl.pallas_call(output_kernel, grid=(7,), in_specs=[tall(2 * NB, F), whole...]
  transfers between devices with their start and end apart: 2 -> 2, of which waited for: 1 -> 1; matrix products, arithmetic and copies ran while one was open for 3% -> 1% of each run, Pallas kernels for 33% -> 20%
where the time goes in v3:
time: 92 us; the launch traced here: 91.5 us
  Pallas kernels  58.9 us (64%)
  starting transfers between devices  18.2 us (20%)
  waiting for transfers between devices  12.2 us (13%)
  local copies, waits for them, and re-layouts  1.03 us (1%)
  other arithmetic  1.01 us (1%)
    pallas_call x1, Pallas kernels, body(): pl.pallas_call(output_kernel, grid=(7,), in_specs=[tall(2 * NB, F), whole...  20 us
    pallas_call x1, Pallas kernels, body(): pl.pallas_call(second_kernel, out_shape=(jax.ShapeDtypeStruct((6 * NB, F)...  18.7 us
    pallas_call x1, Pallas kernels, body(): pl.pallas_call(factor_kernel, out_shape=(jax.ShapeDtypeStruct((PANELS, NB...  18.2 us
    all_to_all x1, waiting for transfers between devices, body(): lead = lax.all_to_all(lead_send, ('row', 'col'), 0, 0, tiled=True)  12.2 us
    all_to_all x1, starting transfers between devices, body(): lead = lax.all_to_all(lead_send, ('row', 'col'), 0, 0, tiled=True)  10.6 us
    all_to_all x1, starting transfers between devices, body(): bulk = lax.all_to_all(bulk_send, ('row', 'col'), 0, 0, tiled=True)  7.53 us
    pallas_call x1, Pallas kernels, body(): pl.pallas_call(pack_kernel, out_shape=(jax.ShapeDtypeStruct((here, F), bf...  2.01 us
  transfers between devices with their start and end apart: 2, of which 1 were waited for; matrix products, arithmetic and copies ran while one was open for 1% of the time, Pallas kernels for 20%

profile of v3, /device:TPU:19, one launch (start us, length us, event | category | flops | bytes accessed | tf_op | source)
XLA Modules:
  0.0 91.5 jit_solution(448413545948723380)
XLA Ops:
  0.0 2.0 %pack.1 = (bf16[128,128]{1,0:T(8,128)(2,1)}, bf16[128,24,128]{2,1,0:T(8,128)(2,1)}) custom-call(f32[128,128]{1,0:T(8,128)} %feat_ref.1, f32[1,128]{1,0:T(1,128)} %bitcast.22, s32[1,128]{1,0:T(1,128)} %bitcast.23), custom_call_target="tpu_custom_call" | custom-call | tf_op jit(solution)/shard_map/pack/pallas_call | solution.py:468
  2.0 0.0 copy-start.2
  2.0 10.6 %all-to-all-start = ((bf16[128,24,128]{2,1,0:T(8,128)(2,1)}), bf16[128,24,128]{2,1,0:T(8,128)(2,1)S(1)}, u32[]{:S(2)}, u32[]{:S(2)}) async-start(bf16[128,24,128]{2,1,0:T(8,128)(2,1)} %get-tuple-element.22), calls=%async_computation | async-start | bytes 1572864 | tf_op jit(solution)/shard_map/all_to_all | solution.py:478
  12.6 0.0 copy-done.2
  12.8 1.0 %pad_maximum_fusion = bf16[128,24,128]{2,1,0:T(8,128)(2,1)} fusion(bf16[128,8,128]{2,1,0:T(8,128)(2,1)S(1)} %bitcast.16, bf16[128,8,128]{2,1,0:T(8,128)(2,1)S(1)} %bitcast.15, bf16[128,8,128]{2,1,0:T(8,128)(2,1)S(1)} %bitcast.17), kind=kLoop, calls=%fused_computation | loop fusion | flops 2359296 | bytes 1572864 | tf_op jit(solution)/shard_map/concatenate | solution.py:483
  13.8 12.2 %all-to-all-done = bf16[128,24,128]{2,1,0:T(8,128)(2,1)S(1)} async-done(((bf16[128,24,128]{2,1,0:T(8,128)(2,1)}), bf16[128,24,128]{2,1,0:T(8,128)(2,1)S(1)}, u32[]{:S(2)}, u32[]{:S(2)}) %all-to-all-start) | async-done | bytes 786464 | tf_op jit(solution)/shard_map/all_to_all | solution.py:478
  26.1 0.0 copy-start
  26.1 7.5 %all-to-all-start.1 = ((bf16[128,24,128]{2,1,0:T(8,128)(2,1)}), bf16[128,24,128]{2,1,0:T(8,128)(2,1)S(1)}, u32[]{:S(2)}, u32[]{:S(2)}) async-start(bf16[128,24,128]{2,1,0:T(8,128)(2,1)} %pad_maximum_fusion), calls=%async_computation.1 | async-start | bytes 1572864 | tf_op jit(solution)/shard_map/all_to_all | solution.py:486
  33.6 0.0 copy-done
  33.6 18.2 %first_panel.1 = (bf16[2,512,256]{2,1,0:T(8,128)(2,1)}, f32[2,8,512]{2,1,0:T(8,128)}, f32[1024,128]{1,0:T(8,128)}, bf16[2,512,512]{2,1,0:T(8,128)(2,1)}, bf16[51...) custom-call(bf16[16,8,24,128]{3,2,1,0:T(8,128)(2,1)} %bitcast.13, ...), custom_call_target="tpu_custom_call" | custom-call | tf_op jit(solution)/shard_map/first_panel/pallas_call | solution.py:488
  51.8 0.0 all-to-all-done.1
  51.8 0.0 copy-start.1
  51.8 0.9 copy-done.1
  52.7 18.7 %second_panel.1 = (bf16[3072,128]{1,0:T(8,128)(2,1)}, f32[1024,128]{1,0:T(8,128)}, bf16[3072,512]{1,0:T(8,128)(2,1)}, bf16[2,512,512]{2,1,0:T(8,128)(2,1)}) custom-call(bf16[16,8,24,128]{3,2,1,0:T(8,128)(2,1)} %bitcast.14, f32[3,8,128]{2,1,0:T(8,128)} %get-tuple-element.25.slots_ref, f32[3,8,128]{2,1,0:T(8,128)} %get-tuple-element.26.noises_ref, ...), custom_call_target="tpu_custom_call" | custom-call | tf_op jit(solution)/shard_map/second_panel/pallas_call | solution.py:511
  71.5 20.0 %output.1 = bf16[1024,2048]{1,0:T(8,128)(2,1)} custom-call(bf16[3072,128]{1,0:T(8,128)(2,1)} %get-tuple-element.32.rows_ref, f32[1024,128]{1,0:T(8,128)} %get-tuple-element.33.row_noise_ref, f32[1,128]{1,0:T(1,128)} %bitcast.21, bf16[2,512,256]{2,1,0:T(8,128)(2,1)} %get-tuple-element.27.right_ref.lead_ref, ...), custom_call_target="tpu_custom_call" | custom-call | tf_op jit(solution)/shard_map/output/pallas_call | solution.py:535
  (4 shorter events, 0.1 us)
Async XLA Ops:
  2.0 10.6 %copy-start.2 = (bf16[128,128]{1,0:T(8,128)(2,1)S(1)}, bf16[128,128]{1,0:T(8,128)(2,1)}, u32[]{:S(2)}) copy-start(bf16[128,128]{1,0:T(8,128)(2,1)} %get-tuple-element.21) | copy-start | bytes 98308
  2.0 24.1 %all-to-all-start = ((bf16[128,24,128]{2,1,0:T(8,128)(2,1)}), bf16[128,24,128]{2,1,0:T(8,128)(2,1)S(1)}, u32[]{:S(2)}, u32[]{:S(2)}) async-start(bf16[128,24,128]{2,1,0:T(8,128)(2,1)} %get-tuple-element.22), calls=%async_computation | async-start | bytes 1572864 | tf_op jit(solution)/shard_map/all_to_all | solution.py:478
  26.1 7.5 %copy-start = (bf16[128,24,128]{2,1,0:T(8,128)(2,1)}, bf16[128,24,128]{2,1,0:T(8,128)(2,1)S(1)}, u32[]{:S(2)}) copy-start(bf16[128,24,128]{2,1,0:T(8,128)(2,1)S(1)} %all-to-all-done) | copy-start | bytes 2359300
  26.1 25.8 %all-to-all-start.1 = ((bf16[128,24,128]{2,1,0:T(8,128)(2,1)}), bf16[128,24,128]{2,1,0:T(8,128)(2,1)S(1)}, u32[]{:S(2)}, u32[]{:S(2)}) async-start(bf16[128,24,128]{2,1,0:T(8,128)(2,1)} %pad_maximum_fusion), calls=%async_computation.1 | async-start | bytes 1572864 | tf_op jit(solution)/shard_map/all_to_all | solution.py:486
  51.8 0.9 copy-start.1

commit v4 on v3

--- a/solution.py
+++ b/solution.py
@@ -1,3 +1,5 @@
+import itertools
+
 import jax
 import jax.numpy as jnp
 from jax import lax
@@ -249,27 +251,50 @@
     return jnp.concatenate(out, axis=0)
 
 
-def invert_panel(a_ref, w_ref, spill_ref, fillers=(None,) * 4):
+def invert_panel(a_ref, w_ref, spill_ref, fillers):
+    def rest(s, w_left, w_right, near):
+        e = s + 128
+        n = e + 128
+        low = near
+        if n < NB:
+            far = split2(nt(left4(split2(a_ref[n:NB, s:e])), w_right))
+            low = [jnp.concatenate([p, q], axis=0) for p, q in zip(near, far)]
+            yield
+            right = right4(low, 1)
+            for i in range(n, NB, 128):
+                left = left4([p[i - e : i - e + 128, :] for p in low])
+                a_ref[i : i + 128, e : i + 128] = a_ref[i : i + 128, e : i + 128] - nt(
+                    left, right[: i + 128 - e, :]
+                )
+                yield
+        if s > 0:
+            w_ref[s:e, 0:s] = nn(w_left, right4(split2(w_ref[s:e, 0:s]), 0))
+            yield
+        if e < NB:
+            w_ref[e:NB, 0:e] = w_ref[e:NB, 0:e] - nn(
+                left4(low), right4(split2(w_ref[s:e, 0:e]), 0)
+            )
+            yield
+
     w_ref[...] = jnp.zeros((NB, NB), f32)
+    block = a_ref[0:128, 0:128]
+    pending = ()
     for s in range(0, NB, 128):
         e = s + 128
-        filler = fillers[s // 128]
-        w = invert_factor(a_ref[s:e, s:e], spill_ref, filler)
-        if filler is not None:
-            for _ in filler:
-                pass
+        filler = itertools.chain(pending, fillers[s // 128])
+        w = invert_factor(block, spill_ref, filler)
+        for _ in filler:
+            pass
+        w_ref[s:e, s:e] = w
         pieces = split2(w)
-        wl = left4(pieces)
+        w_right = right4(pieces, 1)
+        near = None
         if e < NB:
-            low = nt(left4(split2(a_ref[e:NB, s:e])), right4(pieces, 1))
-            low_pieces = split2(low)
-            low_left = left4(low_pieces)
-            a_ref[e:NB, e:NB] = a_ref[e:NB, e:NB] - nt(low_left, right4(low_pieces, 1))
-        if s > 0:
-            w_ref[s:e, 0:s] = nn(wl, right4(split2(w_ref[s:e, 0:s]), 0))
-        w_ref[s:e, s:e] = w
-        if e < NB:
-            w_ref[e:NB, 0:e] = w_ref[e:NB, 0:e] - nn(low_left, right4(split2(w_ref[s:e, 0:e]), 0))
+            near = split2(nt(left4(split2(a_ref[e : e + 128, s:e])), w_right))
+            block = a_ref[e : e + 128, e : e + 128] - nt(left4(near), right4(near, 1))
+        pending = rest(s, left4(pieces), w_right, near)
+    for _ in pending:
+        pass
 
 
 def times_inverse(left, pieces):
@@ -320,79 +345,93 @@
             noises_ref[kind] = spread_rows(noise_table, blocks[2 * kind])
             yield
 
-    invert_panel(a_ref.at[0], inv_ref, spill_ref, (rest(), None, None, None))
+    half = NB // 2
+
+    def first_half():
+        below = split2(a_ref[1, :, :half])
+        p21 = nt(left3(below), right3(split2(inv_ref[:half, :half]))).astype(bf16)
+        p21_ref[:, :half] = p21
+        yield
+        next_ref[...] = a_ref[2] - nt(p21, p21)
+        yield
+
+    invert_panel(a_ref.at[0], inv_ref, spill_ref, (rest(), (), first_half(), ()))
     pieces = split2(inv_ref[...])
     for i in range(2):
         w_ref[i] = pieces[i]
-    p21 = times_inverse(a_ref[1], pieces).astype(bf16)
-    p21_ref[...] = p21
-    next_ref[...] = a_ref[2] - nt(p21, p21)
-
-
-UNIT = 256
-
-
-def second_kernel(
+    p21 = nt(left3(split2(a_ref[1])), right3([p[half:, :] for p in pieces])).astype(bf16)
+    p21_ref[:, half:] = p21
+    next_ref[...] = next_ref[...] - nt(p21, p21)
+
+
+def second_panel(
     bulk_ref, slots_ref, noises_ref, scale_ref, right_ref, norm_ref, lead_noise_ref,
-    w_ref, next_ref, rows_ref, row_noise_ref, p1_ref, w2_ref, a_ref, inv_ref, spill_ref,
+    w_ref, next_ref, rows_ref, row_noise_ref, p_ref, w2_ref, a_ref, inv_ref, spill_ref,
 ):
     a_ref[...] = next_ref[...]
     scale = scale_ref[...]
     half = NB // 2
     blocks = positions()
 
-    def unit(index):
-        block = blocks[index // 2]
-        at = slice(index * UNIT, (index + 1) * UNIT)
-        rows = []
-        for i in range(2):
-            kind, c = divmod(index * 2 + i, 8)
-            hot = one_hot(slots_ref[kind, c : c + 1, :])
-            rows.append(nn(hot, bulk_ref[:, c, 8 * kind : 8 * kind + 8, :].reshape(128, F)))
-            if kind == 0:
-                row_noise_ref[c * 128 : c * 128 + 128, :] = place_noise(
-                    hot, noises_ref[kind, c : c + 1, :]
-                )
-        rows = jnp.concatenate(rows, axis=0).astype(bf16)
-        rows_ref[at, :] = rows
-        yield
-        value = kernel_values(*left_operand(rows, scale), right_ref[0], norm_ref[0])
-        lo = index % 2 * UNIT
-        lead = jnp.where(block == 0, lead_noise_ref[lo : lo + UNIT, :], 0.0)
-        pieces = split2(add_diagonal(value, lead, lo))
-        yield
-        top = nt(
-            left3([p[:, :half] for p in pieces]),
-            right3([w_ref[i, :half, :half] for i in range(2)]),
-        )
-        p1_ref[at, :half] = top.astype(bf16)
-        yield
-        bottom = nt(left3(pieces), right3([w_ref[i, half:, :] for i in range(2)]))
-        p1_ref[at, half:] = bottom.astype(bf16)
-        yield
-
-    def units(first, last):
-        for index in range(first, last):
-            yield from unit(index)
-
-    invert_panel(a_ref, inv_ref, spill_ref, [units(3 * i, 3 * i + 3) for i in range(4)])
+    def units():
+        for tile in range(6):
+            at = slice(tile * NB, (tile + 1) * NB)
+            rows = []
+            for i in range(4):
+                kind, c = divmod(tile * 4 + i, 8)
+                hot = one_hot(slots_ref[kind, c : c + 1, :])
+                rows.append(nn(hot, bulk_ref[:, c, 8 * kind : 8 * kind + 8, :].reshape(128, F)))
+                if kind == 0:
+                    row_noise_ref[c * 128 : c * 128 + 128, :] = place_noise(
+                        hot, noises_ref[kind, c : c + 1, :]
+                    )
+            rows = jnp.concatenate(rows, axis=0).astype(bf16)
+            rows_ref[at, :] = rows
+            yield
+            value = kernel_values(*left_operand(rows, scale), right_ref[0], norm_ref[0])
+            lead = jnp.where(blocks[tile] == 0, lead_noise_ref[:NB, :], 0.0)
+            pieces = split2(add_diagonal(value, lead))
+            yield
+            top = nt(
+                left3([p[:, :half] for p in pieces]),
+                right3([w_ref[i, :half, :half] for i in range(2)]),
+            )
+            p_ref[at, :half] = top.astype(bf16)
+            yield
+            bottom = nt(left3(pieces), right3([w_ref[i, half:, :] for i in range(2)]))
+            p_ref[at, half:NB] = bottom.astype(bf16)
+            yield
+
+    work = units()
+    invert_panel(a_ref, inv_ref, spill_ref, [itertools.islice(work, 6) for _ in range(4)])
+    for _ in work:
+        pass
     pieces = split2(inv_ref[...])
     for i in range(2):
         w2_ref[i] = pieces[i]
 
 
 def output_kernel(
-    rows_ref, row_noise_ref, scale_ref, lead_ref, lead_norm_ref, lead_noise_ref,
-    p1_ref, p21_ref, w_ref, out_ref, p_ref, left_ref, left_norm_ref, right_ref, right_norm_ref,
+    bulk_ref, slots_ref, noises_ref, scale_ref, lead_ref, lead_norm_ref, lead_noise_ref,
+    w1_ref, p21_ref, next_ref, out_ref, rows_ref, row_noise_ref, p_ref, w_ref, a_ref, inv_ref,
+    spill_ref, left_ref, left_norm_ref, right_ref, right_norm_ref,
 ):
-    step = pl.program_id(0)
+    @pl.when(pl.program_id(0) == 0)
+    def _():
+        second_panel(
+            bulk_ref, slots_ref, noises_ref, scale_ref, lead_ref, lead_norm_ref, lead_noise_ref,
+            w1_ref, next_ref, rows_ref, row_noise_ref, p_ref, w_ref, a_ref, inv_ref, spill_ref,
+        )
+
+    step = pl.program_id(0) - 1
     blocks = positions()
     tall = 2 * NB
 
-    @pl.when(step < 3)
+    @pl.when((step >= 0) & (step < 3))
     def _():
         pair = [pick(blocks[i::2], step) for i in range(2)]
-        rows = rows_ref[...]
+        at = pl.multiple_of(step * tall, tall)
+        rows = rows_ref[pl.ds(at, tall), :]
         scale = scale_ref[...]
         left, left_norm = left_operand(rows, scale)
 
@@ -417,11 +456,9 @@
             ],
             axis=0,
         )
-        p1 = p1_ref[...]
+        p1 = p_ref[pl.ds(at, tall), :NB]
         second = value - nt(p1, p21_ref[...])
         p2 = times_inverse(second, [w_ref[i] for i in range(2)])
-        at = pl.multiple_of(step * tall, tall)
-        p_ref[pl.ds(at, tall), :NB] = p1
         for i in range(2):
             kept = jnp.where(pair[i] >= 1, p2[i * NB : (i + 1) * NB, :], 0.0)
             p_ref[pl.ds(at + i * NB, NB), NB:] = kept.astype(bf16)
@@ -508,47 +545,19 @@
         name="first_panel",
     )(lead.reshape(nrows, ncols, 24, F), scale)
 
-    rows, row_noise, p1, w2 = pl.pallas_call(
-        second_kernel,
-        out_shape=(
-            jax.ShapeDtypeStruct((6 * NB, F), bf16),
-            jax.ShapeDtypeStruct((2 * NB, 128), f32),
-            jax.ShapeDtypeStruct((6 * NB, NB), bf16),
-            jax.ShapeDtypeStruct((2, NB, NB), bf16),
-        ),
-        in_specs=[VMEM] * 9,
-        out_specs=(VMEM,) * 4,
+    return pl.pallas_call(
+        output_kernel,
+        grid=(8,),
+        in_specs=[VMEM] * 10,
+        out_specs=pl.BlockSpec((2 * NB, NB), lambda i: (0, jnp.maximum(i - 4, 0))),
         scratch_shapes=[
+            pltpu.VMEM((6 * NB, F), bf16),
+            pltpu.VMEM((2 * NB, 128), f32),
+            pltpu.VMEM((6 * NB, PANELS * NB), bf16),
+            pltpu.VMEM((2, NB, NB), bf16),
             pltpu.VMEM((NB, NB), f32),
             pltpu.VMEM((NB, NB), f32),
             pltpu.VMEM((64, 8, 128), f32),
-        ],
-        compiler_params=PARAMS,
-        name="second_panel",
-    )(
-        bulk.reshape(nrows, ncols, 24, F), slots, noises, scale, right, norm, lead_noise, w1,
-        trailing,
-    )
-
-    whole = lambda *shape: pl.BlockSpec(shape, lambda i: (0,) * len(shape))
-    tall = lambda *shape: pl.BlockSpec(shape, lambda i: (jnp.minimum(i, 2), 0))
-    return pl.pallas_call(
-        output_kernel,
-        grid=(7,),
-        in_specs=[
-            tall(2 * NB, F),
-            whole(2 * NB, 128),
-            whole(1, F),
-            whole(PANELS, NB, 2 * F),
-            whole(PANELS, 8, NB),
-            whole(PANELS * NB, 128),
-            tall(2 * NB, NB),
-            whole(NB, NB),
-            whole(2, NB, NB),
-        ],
-        out_specs=pl.BlockSpec((2 * NB, NB), lambda i: (0, jnp.maximum(i - 3, 0))),
-        scratch_shapes=[
-            pltpu.VMEM((6 * NB, PANELS * NB), bf16),
             pltpu.VMEM((2 * NB, 2 * F), bf16),
             pltpu.VMEM((2 * NB, 128), f32),
             pltpu.VMEM((4, NB, 2 * F), bf16),
@@ -557,7 +566,10 @@
         out_shape=jax.ShapeDtypeStruct((2 * NB, 4 * NB), bf16),
         compiler_params=PARAMS,
         name="output",
-    )(rows, row_noise, scale, right, norm, lead_noise, p1, p21, w2)
+    )(
+        bulk.reshape(nrows, ncols, 24, F), slots, noises, scale, right, norm, lead_noise, w1,
+        p21, trailing,
+    )
 
 
 def solution(mesh):

time: 92 us -> 86.9 us (0.945)
  Pallas kernels: 58.9 us -> 53.8 us
    pallas_call x2 -> x1, Pallas kernels: 38.7 us -> 34.3 us  [body(): pl.pallas_call(output_kernel, grid=(8,), in_specs=[VMEM] * 10, out_specs=...]
where the time goes in v4:
time: 86.9 us; the launch traced here: 86.3 us
  Pallas kernels  53.8 us (62%)
  starting transfers between devices  18.2 us (21%)
  waiting for transfers between devices  12.2 us (14%)
  other arithmetic  1.02 us (1%)
  local copies, waits for them, and re-layouts  1.01 us (1%)
    pallas_call x1, Pallas kernels, body(): pl.pallas_call(output_kernel, grid=(8,), in_specs=[VMEM] * 10, out_specs=...  34.3 us
    pallas_call x1, Pallas kernels, body(): pl.pallas_call(factor_kernel, out_shape=(jax.ShapeDtypeStruct((PANELS, NB...  17.4 us
    all_to_all x1, waiting for transfers between devices, body(): lead = lax.all_to_all(lead_send, ('row', 'col'), 0, 0, tiled=True)  12.2 us
    all_to_all x1, starting transfers between devices, body(): lead = lax.all_to_all(lead_send, ('row', 'col'), 0, 0, tiled=True)  10.6 us
    all_to_all x1, starting transfers between devices, body(): bulk = lax.all_to_all(bulk_send, ('row', 'col'), 0, 0, tiled=True)  7.53 us
    pallas_call x1, Pallas kernels, body(): pl.pallas_call(pack_kernel, out_shape=(jax.ShapeDtypeStruct((here, F), bf...  2.01 us
  transfers between devices with their start and end apart: 2, of which 1 were waited for; matrix products, arithmetic and copies ran while one was open for 1% of the time, Pallas kernels for 20%

profile of v4, /device:TPU:19, one launch (start us, length us, event | category | flops | bytes accessed | tf_op | source)
XLA Modules:
  0.0 86.3 jit_solution(14668058982623579224)
XLA Ops:
  0.0 2.0 %pack.1 = (bf16[128,128]{1,0:T(8,128)(2,1)}, bf16[128,24,128]{2,1,0:T(8,128)(2,1)}) custom-call(f32[128,128]{1,0:T(8,128)} %feat_ref.1, f32[1,128]{1,0:T(1,128)} %bitcast.21, s32[1,128]{1,0:T(1,128)} %bitcast.22), custom_call_target="tpu_custom_call" | custom-call | tf_op jit(solution)/shard_map/pack/pallas_call | solution.py:505
  2.0 0.0 copy-start.2
  2.0 10.6 %all-to-all-start = ((bf16[128,24,128]{2,1,0:T(8,128)(2,1)}), bf16[128,24,128]{2,1,0:T(8,128)(2,1)S(1)}, u32[]{:S(2)}, u32[]{:S(2)}) async-start(bf16[128,24,128]{2,1,0:T(8,128)(2,1)} %get-tuple-element.18), calls=%async_computation | async-start | bytes 1572864 | tf_op jit(solution)/shard_map/all_to_all | solution.py:515
  12.6 0.0 copy-done.2
  12.8 1.0 %pad_maximum_fusion = bf16[128,24,128]{2,1,0:T(8,128)(2,1)} fusion(bf16[128,8,128]{2,1,0:T(8,128)(2,1)S(1)} %bitcast.16, bf16[128,8,128]{2,1,0:T(8,128)(2,1)S(1)} %bitcast.15, bf16[128,8,128]{2,1,0:T(8,128)(2,1)S(1)} %bitcast.17), kind=kLoop, calls=%fused_computation | loop fusion | flops 2359296 | bytes 1572864 | tf_op jit(solution)/shard_map/concatenate | solution.py:520
  13.8 12.2 %all-to-all-done = bf16[128,24,128]{2,1,0:T(8,128)(2,1)S(1)} async-done(((bf16[128,24,128]{2,1,0:T(8,128)(2,1)}), bf16[128,24,128]{2,1,0:T(8,128)(2,1)S(1)}, u32[]{:S(2)}, u32[]{:S(2)}) %all-to-all-start) | async-done | bytes 786464 | tf_op jit(solution)/shard_map/all_to_all | solution.py:515
  26.1 0.0 copy-start.1
  26.1 7.5 %all-to-all-start.1 = ((bf16[128,24,128]{2,1,0:T(8,128)(2,1)}), bf16[128,24,128]{2,1,0:T(8,128)(2,1)S(1)}, u32[]{:S(2)}, u32[]{:S(2)}) async-start(bf16[128,24,128]{2,1,0:T(8,128)(2,1)} %pad_maximum_fusion), calls=%async_computation.1 | async-start | bytes 1572864 | tf_op jit(solution)/shard_map/all_to_all | solution.py:523
  33.6 0.0 copy-done.1
  33.6 17.4 %first_panel.1 = (bf16[2,512,256]{2,1,0:T(8,128)(2,1)}, f32[2,8,512]{2,1,0:T(8,128)}, f32[1024,128]{1,0:T(8,128)}, bf16[2,512,512]{2,1,0:T(8,128)(2,1)}, bf16[51...) custom-call(bf16[16,8,24,128]{3,2,1,0:T(8,128)(2,1)} %bitcast.14, ...), custom_call_target="tpu_custom_call" | custom-call | tf_op jit(solution)/shard_map/first_panel/pallas_call | solution.py:525
  51.1 0.0 all-to-all-done.1
  51.1 0.0 copy-start
  51.1 0.9 %copy-done = bf16[128,24,128]{2,1,0:T(8,128)(2,1)} copy-done((bf16[128,24,128]{2,1,0:T(8,128)(2,1)}, bf16[128,24,128]{2,1,0:T(8,128)(2,1)S(1)}, u32[]{:S(2)}) %copy-start) | copy-done | bytes 786456
  52.0 34.3 %output.1 = bf16[1024,2048]{1,0:T(8,128)(2,1)} custom-call(bf16[16,8,24,128]{3,2,1,0:T(8,128)(2,1)} %bitcast.13, f32[3,8,128]{2,1,0:T(8,128)} %get-tuple-element.21.slots_ref, f32[3,8,128]{2,1,0:T(8,128)} %get-tuple-element.22.noises_ref, f32[1,128]{1,0:T(1,128)} %bitcast.20, bf16[2,512,256]{2,1,0:T(8,128)(2,1)} %get-tuple-element.23.lead_ref, ...), custom_call_target="tpu_custom_call" | custom-call | tf_op jit(solution)/shard_map/output/pallas_call | solution.py:548
  (4 shorter events, 0.1 us)
Async XLA Ops:
  2.0 10.6 %copy-start.2 = (bf16[128,128]{1,0:T(8,128)(2,1)S(1)}, bf16[128,128]{1,0:T(8,128)(2,1)}, u32[]{:S(2)}) copy-start(bf16[128,128]{1,0:T(8,128)(2,1)} %get-tuple-element.17) | copy-start | bytes 98308
  2.0 24.1 %all-to-all-start = ((bf16[128,24,128]{2,1,0:T(8,128)(2,1)}), bf16[128,24,128]{2,1,0:T(8,128)(2,1)S(1)}, u32[]{:S(2)}, u32[]{:S(2)}) async-start(bf16[128,24,128]{2,1,0:T(8,128)(2,1)} %get-tuple-element.18), calls=%async_computation | async-start | bytes 1572864 | tf_op jit(solution)/shard_map/all_to_all | solution.py:515
  26.1 7.5 %copy-start.1 = (bf16[128,24,128]{2,1,0:T(8,128)(2,1)}, bf16[128,24,128]{2,1,0:T(8,128)(2,1)S(1)}, u32[]{:S(2)}) copy-start(bf16[128,24,128]{2,1,0:T(8,128)(2,1)S(1)} %all-to-all-done) | copy-start | bytes 2359300
  26.1 25.0 %all-to-all-start.1 = ((bf16[128,24,128]{2,1,0:T(8,128)(2,1)}), bf16[128,24,128]{2,1,0:T(8,128)(2,1)S(1)}, u32[]{:S(2)}, u32[]{:S(2)}) async-start(bf16[128,24,128]{2,1,0:T(8,128)(2,1)} %pad_maximum_fusion), calls=%async_computation.1 | async-start | bytes 1572864 | tf_op jit(solution)/shard_map/all_to_all | solution.py:523
  51.1 0.9 %copy-start = (bf16[128,24,128]{2,1,0:T(8,128)(2,1)}, bf16[128,24,128]{2,1,0:T(8,128)(2,1)S(1)}, u32[]{:S(2)}) copy-start(bf16[128,24,128]{2,1,0:T(8,128)(2,1)S(1)} %all-to-all-done.1) | copy-start | bytes 2359300

commit v5 on v4

--- a/solution.py
+++ b/solution.py
@@ -122,7 +122,7 @@
 
 
 def place_noise(hot, noises):
-    return nt(hot, jnp.broadcast_to(noises.astype(bf16), hot.shape))
+    return nt(jnp.broadcast_to(noises.astype(bf16), (8, hot.shape[1])), hot)
 
 
 def norm_pieces(rows, scale):
@@ -152,7 +152,7 @@
     for i in range(0, n, 128):
         band = value[i : i + 128, :]
         at = start + i
-        square = band[:, at : at + 128] + jnp.where(eye, noise[i : i + 128, :], 0.0)
+        square = band[:, at : at + 128] + jnp.where(eye, noise[0:1, i : i + 128], 0.0)
         parts = [band[:, :at], square, band[:, at + 128 :]]
         bands.append(jnp.concatenate([p for p in parts if p.shape[1]], axis=1))
     return jnp.concatenate(bands, axis=0)
@@ -321,13 +321,13 @@
             hot = one_hot(slots[c : c + 1, :])
             at = panel * NB + c * 128
             rows.append(nn(hot, lead_ref[:, c, 8 * panel : 8 * panel + 8, :].reshape(128, F)))
-            lead_noise_ref[at : at + 128, :] = place_noise(hot, noises[c : c + 1, :])
+            lead_noise_ref[:, at : at + 128] = place_noise(hot, noises[c : c + 1, :])
         rows = jnp.concatenate(rows, axis=0).astype(bf16)
         right_ref[panel], norm_ref[panel] = right_operand(rows, scale)
         return left_operand(rows, scale)
 
     a_ref[0] = add_diagonal(
-        kernel_values(*lead_rows(0), right_ref[0], norm_ref[0]), lead_noise_ref[:NB, :]
+        kernel_values(*lead_rows(0), right_ref[0], norm_ref[0]), lead_noise_ref[:, :NB]
     )
 
     def rest():
@@ -336,7 +336,7 @@
         a_ref[1] = kernel_values(*left, right_ref[0], norm_ref[0])
         yield
         a_ref[2] = add_diagonal(
-            kernel_values(*left, right_ref[1], norm_ref[1]), lead_noise_ref[NB:, :]
+            kernel_values(*left, right_ref[1], norm_ref[1]), lead_noise_ref[:, NB:]
         )
         yield
         blocks = positions()
@@ -382,14 +382,14 @@
                 hot = one_hot(slots_ref[kind, c : c + 1, :])
                 rows.append(nn(hot, bulk_ref[:, c, 8 * kind : 8 * kind + 8, :].reshape(128, F)))
                 if kind == 0:
-                    row_noise_ref[c * 128 : c * 128 + 128, :] = place_noise(
+                    row_noise_ref[:, c * 128 : c * 128 + 128] = place_noise(
                         hot, noises_ref[kind, c : c + 1, :]
                     )
             rows = jnp.concatenate(rows, axis=0).astype(bf16)
             rows_ref[at, :] = rows
             yield
             value = kernel_values(*left_operand(rows, scale), right_ref[0], norm_ref[0])
-            lead = jnp.where(blocks[tile] == 0, lead_noise_ref[:NB, :], 0.0)
+            lead = jnp.where(blocks[tile] == 0, lead_noise_ref[:, :NB], 0.0)
             pieces = split2(add_diagonal(value, lead))
             yield
             top = nt(
@@ -448,7 +448,7 @@
                 right_norm_ref[2 * step - 2 + i] = norm[:, i * NB : (i + 1) * NB]
 
         value = kernel_values(left, left_norm, lead_ref[1], lead_norm_ref[1])
-        noise = lead_noise_ref[NB:, :]
+        noise = lead_noise_ref[:, NB:]
         value = jnp.concatenate(
             [
                 add_diagonal(value[i * NB : (i + 1) * NB, :], jnp.where(pair[i] == 1, noise, 0.0))
@@ -483,7 +483,7 @@
             at = pl.multiple_of((2 + j) * NB, NB)
             value = value - nt(p_ref[:tall, :], p_ref[pl.ds(at, NB), :])
             for i in range(2):
-                noise = row_noise_ref[i * NB : (i + 1) * NB, :]
+                noise = row_noise_ref[:, i * NB : (i + 1) * NB]
                 noise = jnp.where(blocks[i] == col_block, noise, 0.0)
                 half = add_diagonal(value[i * NB : (i + 1) * NB, :], noise)
                 half = jnp.where(blocks[i] >= PANELS, half, 0.0)
@@ -492,7 +492,7 @@
 
 VMEM = pl.BlockSpec(memory_space=pltpu.VMEM)
 SMEM = pl.BlockSpec(memory_space=pltpu.SMEM)
-PARAMS = pltpu.CompilerParams(vmem_limit_bytes=56 * 1024 * 1024)
+PARAMS = pltpu.CompilerParams(vmem_limit_bytes=44 * 1024 * 1024)
 
 
 def body(features, noise, owner_slot, inv_length):
@@ -522,16 +522,17 @@
     bulk_send, lead = lax.optimization_barrier((bulk_send, lead))
     bulk = lax.all_to_all(bulk_send, ("row", "col"), 0, 0, tiled=True)
 
+    lead = pltpu.with_memory_space_constraint(lead.reshape(nrows, ncols, 24, F), pltpu.VMEM)
     right, norm, lead_noise, w1, p21, slots, noises, trailing = pl.pallas_call(
         factor_kernel,
         out_shape=(
-            jax.ShapeDtypeStruct((PANELS, NB, 2 * F), bf16),
-            jax.ShapeDtypeStruct((PANELS, 8, NB), f32),
-            jax.ShapeDtypeStruct((PANELS * NB, 128), f32),
+            pltpu.VMEM((PANELS, NB, 2 * F), bf16),
+            pltpu.VMEM((PANELS, 8, NB), f32),
+            pltpu.VMEM((8, PANELS * NB), f32),
             jax.ShapeDtypeStruct((2, NB, NB), bf16),
             jax.ShapeDtypeStruct((NB, NB), bf16),
-            jax.ShapeDtypeStruct((3, 8, here), f32),
-            jax.ShapeDtypeStruct((3, 8, here), f32),
+            pltpu.VMEM((3, 8, here), f32),
+            pltpu.VMEM((3, 8, here), f32),
             jax.ShapeDtypeStruct((NB, NB), f32),
         ),
         in_specs=[VMEM] * 2,
@@ -543,8 +544,13 @@
         ],
         compiler_params=PARAMS,
         name="first_panel",
-    )(lead.reshape(nrows, ncols, 24, F), scale)
-
+    )(lead, scale)
+
+    keep = lambda x: pltpu.with_memory_space_constraint(x, pltpu.VMEM)
+    bulk = keep(bulk.reshape(nrows, ncols, 24, F))
+    slots, noises, right, norm, lead_noise = map(
+        keep, (slots, noises, right, norm, lead_noise)
+    )
     return pl.pallas_call(
         output_kernel,
         grid=(8,),
@@ -552,7 +558,7 @@
         out_specs=pl.BlockSpec((2 * NB, NB), lambda i: (0, jnp.maximum(i - 4, 0))),
         scratch_shapes=[
             pltpu.VMEM((6 * NB, F), bf16),
-            pltpu.VMEM((2 * NB, 128), f32),
+            pltpu.VMEM((8, 2 * NB), f32),
             pltpu.VMEM((6 * NB, PANELS * NB), bf16),
             pltpu.VMEM((2, NB, NB), bf16),
             pltpu.VMEM((NB, NB), f32),
@@ -567,8 +573,7 @@
         compiler_params=PARAMS,
         name="output",
     )(
-        bulk.reshape(nrows, ncols, 24, F), slots, noises, scale, right, norm, lead_noise, w1,
-        p21, trailing,
+        bulk, slots, noises, scale, right, norm, lead_noise, w1, p21, trailing
     )
 
 

time: 86.9 us -> 85.4 us (0.983)
  Pallas kernels: 53.8 us -> 49.1 us
  local copies, waits for them, and re-layouts: 1.01 us -> 4.19 us
    unnamed x6 -> x12, local copies, waits for them, and re-layouts: 0.88 us -> 4.06 us
    pallas_call x1, Pallas kernels: 17.4 us -> 14.9 us  [body(): pl.pallas_call(factor_kernel, out_shape=(pltpu.VMEM((PANELS, NB, 2 * F),...]
    pallas_call x1, Pallas kernels: 34.3 us -> 32.2 us  [body(): pl.pallas_call(output_kernel, grid=(8,), in_specs=[VMEM] * 10, out_specs=...]
  transfers between devices with their start and end apart: 2 -> 2, of which waited for: 1 -> 1; matrix products, arithmetic and copies ran while one was open for 1% -> 1% of each run, Pallas kernels for 20% -> 18%
where the time goes in v5:
time: 85.4 us; the launch traced here: 84.8 us
  Pallas kernels  49.1 us (57%)
  starting transfers between devices  18.2 us (21%)
  waiting for transfers between devices  12.2 us (14%)
  local copies, waits for them, and re-layouts  4.19 us (5%)
  other arithmetic  1.02 us (1%)
    pallas_call x1, Pallas kernels, body(): pl.pallas_call(output_kernel, grid=(8,), in_specs=[VMEM] * 10, out_specs=...  32.2 us
    pallas_call x1, Pallas kernels, body(): pl.pallas_call(factor_kernel, out_shape=(pltpu.VMEM((PANELS, NB, 2 * F),...  14.9 us
    all_to_all x1, waiting for transfers between devices, body(): lead = lax.all_to_all(lead_send, ('row', 'col'), 0, 0, tiled=True)  12.2 us
    all_to_all x1, starting transfers between devices, body(): lead = lax.all_to_all(lead_send, ('row', 'col'), 0, 0, tiled=True)  10.6 us
    all_to_all x1, starting transfers between devices, body(): bulk = lax.all_to_all(bulk_send, ('row', 'col'), 0, 0, tiled=True)  7.53 us
    unnamed x12, local copies, waits for them, and re-layouts  4.06 us
    pallas_call x1, Pallas kernels, body(): pl.pallas_call(pack_kernel, out_shape=(jax.ShapeDtypeStruct((here, F), bf...  2.01 us
  transfers between devices with their start and end apart: 2, of which 1 were waited for; matrix products, arithmetic and copies ran while one was open for 1% of the time, Pallas kernels for 18%

profile of v5, /device:TPU:19, one launch (start us, length us, event | category | flops | bytes accessed | tf_op | source)
XLA Modules:
  0.0 84.8 jit_solution(10269919195779435955)
XLA Ops:
  0.0 2.0 %pack.1 = (bf16[128,128]{1,0:T(8,128)(2,1)}, bf16[128,24,128]{2,1,0:T(8,128)(2,1)}) custom-call(f32[128,128]{1,0:T(8,128)} %feat_ref.1, f32[1,128]{1,0:T(1,128)} %bitcast.21, s32[1,128]{1,0:T(1,128)} %bitcast.22), custom_call_target="tpu_custom_call" | custom-call | tf_op jit(solution)/shard_map/pack/pallas_call | solution.py:505
  2.0 0.0 copy-start.5
  2.0 10.6 %all-to-all-start = ((bf16[128,24,128]{2,1,0:T(8,128)(2,1)}), bf16[128,24,128]{2,1,0:T(8,128)(2,1)S(1)}, u32[]{:S(2)}, u32[]{:S(2)}) async-start(bf16[128,24,128]{2,1,0:T(8,128)(2,1)} %get-tuple-element.18), calls=%async_computation | async-start | bytes 1572864 | tf_op jit(solution)/shard_map/all_to_all | solution.py:515
  12.6 0.0 copy-done.5
  12.8 0.0 copy-start.4
  12.8 1.0 %pad_maximum_fusion = bf16[128,24,128]{2,1,0:T(8,128)(2,1)} fusion(bf16[128,8,128]{2,1,0:T(8,128)(2,1)S(1)} %bitcast.18, bf16[128,8,128]{2,1,0:T(8,128)(2,1)S(1)} %bitcast.17, bf16[128,8,128]{2,1,0:T(8,128)(2,1)S(1)} %bitcast.19), kind=kLoop, calls=%fused_computation | loop fusion | flops 2359296 | bytes 1572864 | tf_op jit(solution)/shard_map/concatenate | solution.py:520
  13.8 12.2 %all-to-all-done = bf16[128,24,128]{2,1,0:T(8,128)(2,1)S(1)} async-done(((bf16[128,24,128]{2,1,0:T(8,128)(2,1)}), bf16[128,24,128]{2,1,0:T(8,128)(2,1)S(1)}, u32[]{:S(2)}, u32[]{:S(2)}) %all-to-all-start) | async-done | bytes 786464 | tf_op jit(solution)/shard_map/all_to_all | solution.py:515
  26.1 7.5 %all-to-all-start.1 = ((bf16[128,24,128]{2,1,0:T(8,128)(2,1)}), bf16[128,24,128]{2,1,0:T(8,128)(2,1)S(1)}, u32[]{:S(2)}, u32[]{:S(2)}) async-start(bf16[128,24,128]{2,1,0:T(8,128)(2,1)} %pad_maximum_fusion), calls=%async_computation.1 | async-start | bytes 1572864 | tf_op jit(solution)/shard_map/all_to_all | solution.py:523
  33.6 0.0 copy-done.4
  33.6 14.9 %first_panel.1 = (bf16[2,512,256]{2,1,0:T(8,128)(2,1)S(1)}, f32[2,8,512]{2,1,0:T(8,128)S(1)}, f32[8,1024]{1,0:T(8,128)S(1)}, bf16[2,512,512]{2,1,0:T(8,128)(2,1)...) custom-call(bf16[16,8,24,128]{3,2,1,0:T(8,128)(2,1)S(1)} %bitcast.14, ...), custom_call_target="tpu_custom_call" | custom-call | tf_op jit(solution)/shard_map/first_panel/pallas_call | solution.py:526
  48.5 0.0 copy-start
  48.6 1.0 %copy-done = f32[512,512]{1,0:T(8,128)} copy-done((f32[512,512]{1,0:T(8,128)}, f32[512,512]{1,0:T(8,128)S(1)}, u32[]{:S(2)}) %copy-start) | copy-done | bytes 1048600
  49.5 0.0 copy-start.2
  49.5 0.8 copy-done.2
  50.3 0.0 all-to-all-done.1
  50.3 0.0 copy-start.1
  50.3 1.2 %copy-done.1 = f32[512,512]{1,0:T(8,128)S(1)} copy-done((f32[512,512]{1,0:T(8,128)S(1)}, f32[512,512]{1,0:T(8,128)}, u32[]{:S(2)}) %copy-start.1) | copy-done | bytes 1048600
  51.6 0.0 copy-start.3
  51.6 1.0 %copy-done.3 = bf16[512,512]{1,0:T(8,128)(2,1)S(1)} copy-done((bf16[512,512]{1,0:T(8,128)(2,1)S(1)}, bf16[512,512]{1,0:T(8,128)(2,1)}, u32[]{:S(2)}) %copy-start.3) | copy-done | bytes 524312
  52.6 32.2 %output.1 = bf16[1024,2048]{1,0:T(8,128)(2,1)} custom-call(bf16[16,8,24,128]{3,2,1,0:T(8,128)(2,1)S(1)} %bitcast.13, f32[3,8,128]{2,1,0:T(8,128)S(1)} %get-tuple-element.21.slots_ref, f32[3,8,128]{2,1,0:T(8,128)S(1)} %get-tuple-element.22.noises_ref, f32[1,128]{1,0:T(1,128)S(1)} %bitcast.16, bf16[2,512,256]{2,1,0:T(8,128)(2,1)S(1)} %get-tuple-element.23.lead_ref, ...), custom_call_target="tpu_custom_call" | custom-call | tf_op jit(solution)/shard_map/output/pallas_call | solution.py:554
  (4 shorter events, 0.1 us)
Async XLA Ops:
  2.0 10.6 %copy-start.5 = (bf16[128,128]{1,0:T(8,128)(2,1)S(1)}, bf16[128,128]{1,0:T(8,128)(2,1)}, u32[]{:S(2)}) copy-start(bf16[128,128]{1,0:T(8,128)(2,1)} %get-tuple-element.17) | copy-start | bytes 98308
  2.0 24.1 %all-to-all-start = ((bf16[128,24,128]{2,1,0:T(8,128)(2,1)}), bf16[128,24,128]{2,1,0:T(8,128)(2,1)S(1)}, u32[]{:S(2)}, u32[]{:S(2)}) async-start(bf16[128,24,128]{2,1,0:T(8,128)(2,1)} %get-tuple-element.18), calls=%async_computation | async-start | bytes 1572864 | tf_op jit(solution)/shard_map/all_to_all | solution.py:515
  12.8 20.8 %copy-start.4 = (f32[128]{0:T(128)S(1)}, f32[128]{0:T(128)}, u32[]{:S(2)}) copy-start(f32[128]{0:T(128)} %param.7) | copy-start | bytes 1540
  26.1 24.3 %all-to-all-start.1 = ((bf16[128,24,128]{2,1,0:T(8,128)(2,1)}), bf16[128,24,128]{2,1,0:T(8,128)(2,1)S(1)}, u32[]{:S(2)}, u32[]{:S(2)}) async-start(bf16[128,24,128]{2,1,0:T(8,128)(2,1)} %pad_maximum_fusion), calls=%async_computation.1 | async-start | bytes 1572864 | tf_op jit(solution)/shard_map/all_to_all | solution.py:523
  48.5 1.0 %copy-start = (f32[512,512]{1,0:T(8,128)}, f32[512,512]{1,0:T(8,128)S(1)}, u32[]{:S(2)}) copy-start(f32[512,512]{1,0:T(8,128)S(1)} %get-tuple-element.28.next_ref) | copy-start | bytes 3145732
  49.5 0.8 copy-start.2
  50.3 1.2 %copy-start.1 = (f32[512,512]{1,0:T(8,128)S(1)}, f32[512,512]{1,0:T(8,128)}, u32[]{:S(2)}) copy-start(f32[512,512]{1,0:T(8,128)} %copy-done) | copy-start | bytes 3145732
  51.6 1.0 %copy-start.3 = (bf16[512,512]{1,0:T(8,128)(2,1)S(1)}, bf16[512,512]{1,0:T(8,128)(2,1)}, u32[]{:S(2)}) copy-start(bf16[512,512]{1,0:T(8,128)(2,1)} %copy-done.2) | copy-start | bytes 1572868
